TPU v7x, 32 devices: a whole 2x2x4 slice. The times are simulated.
32 devices in a mesh: groups: 2 (over x), dom: 16 (over z, y, core).
Axes of the slice: x: 2, y: 2, z: 4, core: 2. Of those that a mesh axis runs over, the one named last changes fastest.
Arguments:
- features: bfloat16 [4, 32768, 256], P('groups', 'dom'), parts along dimension 0, may hold values from -6 to 6
- cotangent: bfloat16 [4, 32768, 256], P('groups', 'dom'), parts along dimension 0, may hold values from -6 to 6
- adjacency: bfloat16 [256, 4, 128, 128], P('dom'), may hold values from -0.25 to 0.25
- tile_cols: int32 [256, 4], P('dom'), may hold values from 0 to 255, as said below
- tile_counts: int32 [256], P('dom'), may hold values from 1 to 4, as said below
- w_self: bfloat16 [256, 256], replicated, may hold values from -0.375 to 0.375
- w_neigh: bfloat16 [256, 256], replicated, may hold values from -0.375 to 0.375
- w_out: bfloat16 [256, 256], replicated, may hold values from -0.375 to 0.375
Outputs:
- updated: bfloat16 [4, 32768, 256], P('groups', 'dom'), parts along dimension 0
- grad_features: bfloat16 [4, 32768, 256], P('groups', 'dom'), parts along dimension 0
- grad_self: float32 [512, 256], P('groups'), parts along dimension 0
- grad_neigh: float32 [512, 256], P('groups'), parts along dimension 0
- grad_out: float32 [512, 256], P('groups'), parts along dimension 0
There are 2 independent parts, one for each index of `groups`. A program takes and returns all parts, laid end to end along the dimension named above; an argument that names none is the same for every part. Nothing has to cross between parts.
Inputs may be any that keep to these rules, and one draw needn't show every extreme that they name: tile_cols[r, k] - r lies between -4 and 4 (both reached); block rows of even index have tile_cols[r, 0] = min(r + 4, 255), odd ones max(r - 4, 0); a block column may repeat in a row. `tile_counts`: block rows whose index is a multiple of 3 have 4 live slots.
All inputs are finite; a program needn't handle non-finite values.
Results may differ from a plain program's by a relative error of at most 0.0054.
Values may be sent and summed in bfloat16 or wider, within the bound.
No kernel may reach another device: no remote copies, remote signals or barrier semaphores. Data moves between devices by JAX's collectives and lax.ppermute only.
A program may use at most 128 MiB of HBM per device.

v0:
```python
import math

import jax
import jax.numpy as jnp
from jax import lax
from jax.sharding import PartitionSpec as P

R = 4


def padded(shard, sides, width):
    for axis, dim in sides:
        size, length = (lax.axis_size(axis), shard.shape[dim])
        up = [(i, (i + 1) % size) for i in range(size - 1)]
        down = [(j, i) for i, j in up]
        last = lax.slice_in_dim(shard, length - width, length, axis=dim)
        first = lax.slice_in_dim(shard, 0, width, axis=dim)
        before = lax.ppermute(last, axis, up)
        after = lax.ppermute(first, axis, down)
        shard = jnp.concatenate([before, shard, after], axis=dim)
    return shard


def shifted(value, axis, steps):
    count = lax.axis_size(axis)
    first, last = (max(0, -steps), min(count, count - steps))
    return lax.ppermute(value, axis, [(source, source + steps) for source in range(first, last)])


def fold_rows(contrib_rows, targets, width):
    one_hot = (targets[:, None] == jnp.arange(width, dtype=jnp.int32)[None, :]).astype(jnp.float32)
    return jnp.einsum("ms,cmjf->csjf", one_hot, contrib_rows, precision=lax.Precision.HIGHEST)


def body(features, cotangent, adjacency, tile_cols, tile_counts, w_self, w_neigh, w_out):
    clones, node_rows, hidden = features.shape
    per_device = adjacency.shape[0]
    slots = adjacency.shape[1]
    block_size = adjacency.shape[2]
    first_block = lax.axis_index("dom") * per_device
    slot_ids = jnp.arange(slots, dtype=jnp.int32)
    live_mask = slot_ids[None, :] < tile_counts[:, None]
    live_tiles = jnp.where(live_mask[:, :, None, None], adjacency, jnp.zeros((), jnp.bfloat16))
    extended = padded(features, (("dom", 1),), R * block_size)
    ext_blocks = extended.reshape(clones, per_device + 2 * R, block_size, hidden)
    local_index = tile_cols - first_block + R
    picked = jnp.take(ext_blocks, local_index, axis=1)
    aggregate = jnp.einsum(
        "rkij,crkjf->crif", live_tiles, picked, preferred_element_type=jnp.float32
    )
    aggregate = aggregate.astype(jnp.bfloat16).reshape(clones * node_rows, hidden)
    flat_state = features.reshape(clones * node_rows, hidden)
    pre = jnp.dot(flat_state, w_self, preferred_element_type=jnp.float32) + jnp.dot(
        aggregate, w_neigh, preferred_element_type=jnp.float32
    )
    sigma = jax.nn.sigmoid(pre)
    activated = (pre * sigma).astype(jnp.bfloat16)
    updated = (
        flat_state.astype(jnp.float32)
        + jnp.dot(activated, w_out, preferred_element_type=jnp.float32)
    ).astype(jnp.bfloat16)
    flat_cot = cotangent.reshape(clones * node_rows, hidden)
    grad_act = jnp.dot(flat_cot, w_out.T, preferred_element_type=jnp.float32)
    d_pre = (grad_act * sigma * (1.0 + pre * (1.0 - sigma))).astype(jnp.bfloat16)
    sum_out, sum_self, sum_neigh = lax.psum(
        (
            jnp.dot(activated.T, flat_cot, preferred_element_type=jnp.float32),
            jnp.dot(flat_state.T, d_pre, preferred_element_type=jnp.float32),
            jnp.dot(aggregate.T, d_pre, preferred_element_type=jnp.float32),
        ),
        "dom",
    )
    factor = 1.0 / math.sqrt(2.0 * node_rows * lax.axis_size("dom"))
    d_aggregate = jnp.dot(d_pre, w_neigh.T, preferred_element_type=jnp.float32).astype(jnp.bfloat16)
    direct = flat_cot.astype(jnp.float32) + jnp.dot(
        d_pre, w_self.T, preferred_element_type=jnp.float32
    )
    d_blocks = d_aggregate.reshape(clones, per_device, block_size, hidden)
    contrib = jnp.einsum(
        "rkij,crif->crkjf", live_tiles, d_blocks, preferred_element_type=jnp.float32
    )
    summed = fold_rows(
        contrib.reshape(clones, per_device * slots, block_size, hidden),
        local_index.reshape(-1),
        per_device + 2 * R,
    )
    from_below = shifted(summed[:, per_device + R :].astype(jnp.bfloat16), "dom", 1)
    from_above = shifted(summed[:, :R].astype(jnp.bfloat16), "dom", -1)
    center = summed[:, R : R + per_device]
    center = center.at[:, :R].add(from_below.astype(jnp.float32))
    center = center.at[:, per_device - R :].add(from_above.astype(jnp.float32))
    grad_features = (direct + center.reshape(clones * node_rows, hidden)).astype(jnp.bfloat16)
    return (
        updated.reshape(clones, node_rows, hidden),
        grad_features.reshape(clones, node_rows, hidden),
        sum_self * factor,
        sum_neigh * factor,
        sum_out * factor,
    )


def solution(mesh):
    return jax.shard_map(
        body,
        mesh=mesh,
        in_specs=(
            P("groups", "dom", None),
            P("groups", "dom", None),
            P("dom", None, None, None),
            P("dom", None),
            P("dom"),
            P(),
            P(),
            P(),
        ),
        out_specs=(
            P("groups", "dom", None),
            P("groups", "dom", None),
            P("groups", None),
            P("groups", None),
            P("groups", None),
        ),
        check_vma=False,
    )
```

profile of v0, /device:TPU:0, one launch (start us, length us, event | category | flops | bytes accessed | tf_op | source)
XLA Modules:
  0.0 223.0 jit_solution(15104539682653707110)
XLA Ops:
  7.2 2.2 fusion.33
  9.5 2.4 %collective-permute-start = (bf16[2,512,256]{2,1,0:T(8,128)(2,1)}, bf16[2,512,256]{2,1,0:T(8,128)(2,1)S(1)}, u32[]{:S(2)}, u32[]{:S(2)}) collective-permute-start(bf16[2,512,256]{2,1,0:T(8,128)(2,1)} %get-tuple-element.46), channel_id=1, source_target_pairs={{0,1},{1,2},{2,3},{3,4},{4,5},{5,6},{6,7},{7,8},{8,9},{9,10},{10,1... | collective-permute-start | bytes 1572872 | tf_op jit(solution)/shard_map/ppermute | solution.py:18
  15.7 3.7 %fusion.35 = f32[4096,256]{1,0:T(8,128)} fusion(bf16[4096,256]{1,0:T(8,128)(2,1)S(1)} %bitcast.73, bf16[256,256]{1,0:T(8,128)(2,1)} %param.17), kind=kOutput, calls=%fused_computation.53 | convolution fusion | flops 536870912 | bytes 6422528 | tf_op jit(solution)/shard_map/dot_general | solution.py:53
  21.6 5.6 %gather_fusion = bf16[64,2,128,256]{3,2,1,0:T(8,128)(2,1)} fusion(bf16[2,24,128,256]{3,2,1,0:T(8,128)(2,1)S(1)} %bitcast.72, s32[1024]{0:T(1024)S(1)} %pad_clamp_fusion), kind=kCustom, calls=%fused_computation | custom fusion | bytes 16777472 | tf_op jit(solution)/shard_map/jit(_take)/gather | solution.py:47
  27.2 5.9 %fusion.14 = bf16[2,16,128,256]{3,2,0,1:T(8,128)(2,1)S(1)} fusion(bf16[16,4,2,128,256]{4,3,2,1,0:T(8,128)(2,1)} %bitcast.77, pred[16,4]{1,0:T(8,128)(4,1)S(1)} %copy.23, bf16[16,4,128,128]{3,2,1,0:T(8,128)(2,1)} %param.14, pred[16,4]{1,0:T(8,128)(4,1)S(1)} %iota_compare_fusion.1), kind=kOutput, calls=%fused_computation.24 | convolution fusion | flops 1080033280 | bytes 12583040 | tf_op jit(solution)/shard_map/rkij,crkjf->crif/dot_general | solution.py:48
  33.3 2.0 copy-done.8
  35.3 1.5 multiply_convert_fusion
  36.9 1.8 fusion.8
  38.7 1.7 fusion.36
  42.6 2.1 convolution_convert_fusion
  44.7 1.7 fusion.37
  46.3 10.4 %convolution_bitcast_fusion = f32[2,16,4,128,256]{3,4,2,0,1:T(8,128)} fusion(bf16[2,16,128,256,1]{3,2,1,0,4:T(8,128)(2,1)} %bitcast.76, bf16[16,4,128,128]{3,2,1,0:T(8,128)(2,1)} %param.14, pred[16,4]{1,0:T(8,128)(4,1)S(1)} %iota_compare_fusion.1), kind=kOutput, calls=%fused_computation.3 | convolution fusion | flops 1074790400 | bytes 20971584 | tf_op jit(solution)/shard_map/rkij,crif->crkjf/dot_general | solution.py:79
  56.7 18.0 %copy.28 = f32[2,16,4,128,256]{4,3,2,1,0:T(8,128)} copy(f32[2,16,4,128,256]{3,4,2,0,1:T(8,128)} %convolution_bitcast_fusion) | data formatting | bytes 33554432 | tf_op jit(solution)/shard_map/rkij,crif->crkjf/transpose | solution.py:79
  74.7 22.7 %fusion.34 = (bf16[2,24,128,256]{3,1,2,0:T(8,128)(2,1)}, f32[2,24,128,256]{3,1,2,0:T(8,128)}) fusion(s32[64]{0:T(128)S(1)} %eq.15, f32[2,64,128,256]{3,2,1,0:T(8,128)} %bitcast.71), kind=kOutput, calls=%fused_computation.52 | convolution fusion | flops 1209533952 | bytes 26214656 | tf_op jit(solution)/shard_map/ms,cmjf->csjf/dot_general | solution.py:32
  97.4 2.9 %fusion.32 = (bf16[2,4,128,256]{3,1,2,0:T(4,128)(2,1)S(1)}, bf16[2,4,128,256]{3,1,2,0:T(4,128)(2,1)}) fusion(bf16[2,24,128,256]{3,1,2,0:T(8,128)(2,1)} %get-tuple-element.50), kind=kLoop, calls=%fused_computation.50 | loop fusion | bytes 2097152 | tf_op jit(solution)/shard_map/slice | solution.py:88
  100.3 9.2 %collective-permute-start.2 = (bf16[2,4,128,256]{3,1,2,0:T(4,128)(2,1)}, bf16[2,4,128,256]{3,1,2,0:T(4,128)(2,1)S(1)}, u32[]{:S(2)}, u32[]{:S(2)}) collective-permute-start(bf16[2,4,128,256]{3,1,2,0:T(4,128)(2,1)} %get-tuple-element.45), channel_id=1, source_target_pairs={{0,1},{1,2},{2,3},{3,4},{4,5},{5,6},{6,7},{7,8},{8,9},{9,10},{10,1... | collective-permute-start | bytes 1572872 | tf_op jit(solution)/shard_map/ppermute | solution.py:27
  109.5 2.1 fusion.7
  111.6 1.5 collective-permute-start.3
  113.1 2.5 %slice.85 = f32[2,16,128,256]{3,1,2,0:T(8,128)} slice(f32[2,24,128,256]{3,1,2,0:T(8,128)S(1)} %copy-done.5), slice={[0:2], [4:20], [0:128], [0:256]} | slice | bytes 8388608 | tf_op jit(solution)/shard_map/slice | solution.py:89
  115.6 82.9 %all-reduce.3.cloned.1.call-done = (f32[256,256]{0,1:T(8,128)}, f32[256,256]{0,1:T(8,128)}, f32[256,256]{0,1:T(8,128)}) async-done(((f32[256,256]{0,1:T(8,128)}, f32[256,256]{0,1:T(8,128)}, f32[256,256]{0,1:T(8,128)}), (f32[256,256]{0,1:T(8,128)}, f32[256,256]{0,1:T(8,128)}, f32[256,256]{0,1:T(8,128)})) %all-reduce.3.cloned.1.call-update) | async-done | bytes 786448 | tf_op jit(solution)/shard_map/psum | solution.py:65
  203.1 3.0 %fusion.23 = f32[2,16,128,256]{3,1,2,0:T(8,128)} fusion(f32[2,16,128,256]{3,1,2,0:T(8,128)} %slice.85, f32[2,24,128,256]{3,1,2,0:T(8,128)} %get-tuple-element.51, bf16[2,4,128,256]{3,1,2,0:T(4,128)(2,1)S(1)} %collective-permute-done.2), kind=kLoop, calls=%fused_computation.33 | loop fusion | flops 524288 | bytes 2621440 | tf_op jit(solution)/shard_map/scatter-add | solution.py:90
  206.0 3.0 %fusion.22 = f32[2,16,128,256]{3,1,2,0:T(8,128)} fusion(f32[2,16,128,256]{3,1,2,0:T(8,128)} %fusion.23, bf16[2,4,128,256]{3,1,2,0:T(4,128)(2,1)S(1)} %collective-permute-done.3), kind=kLoop, calls=%fused_computation.31 | loop fusion | flops 524288 | bytes 2621440 | tf_op jit(solution)/shard_map/scatter-add | solution.py:91
  209.0 4.8 %copy.31 = f32[2,16,128,256]{3,2,1,0:T(8,128)S(1)} copy(f32[2,16,128,256]{3,1,2,0:T(8,128)} %fusion.22) | data formatting | bytes 8388608 | tf_op jit(solution)/shard_map/scatter-add | solution.py:91
  213.8 2.3 %fusion.9 = bf16[4096,256]{1,0:T(8,128)(2,1)} fusion(f32[2,16,128,256]{3,2,1,0:T(8,128)S(1)} %copy.31, bf16[4096,256]{1,0:T(8,128)(2,1)S(1)} %copy-done.7, bf16[256,256]{1,0:T(8,128)(2,1)S(1)} %copy-done.14, bf16[4096,256]{1,0:T(8,128)(2,1)S(1)} %bitcast.83), kind=kOutput, calls=%fused_computation.18 | convolution fusion | flops 541065216 | bytes 10616832 | tf_op jit(solution)/shard_map/dot_general | solution.py:75
  (55 shorter events, 13.1 us)
Async XLA Ops:
  7.2 26.1 %copy-start = (bf16[256,256]{1,0:T(8,128)(2,1)S(1)}, bf16[256,256]{1,0:T(8,128)(2,1)}, u32[]{:S(2)}) copy-start(bf16[256,256]{1,0:T(8,128)(2,1)} %param.18) | copy-start | bytes 393220
  7.2 8.5 %copy-start.2 = (bf16[2,2048,256]{2,1,0:T(8,128)(2,1)S(1)}, bf16[2,2048,256]{2,1,0:T(8,128)(2,1)}, u32[]{:S(2)}) copy-start(bf16[2,2048,256]{2,1,0:T(8,128)(2,1)} %param.12) | copy-start | bytes 6291460
  7.2 191.3 %all-reduce.3.cloned.1.call-start = ((), (), s32[]{:S(2)}) async-start(), calls=%async_computation | async-start | bytes 1572864 | tf_op jit(solution)/shard_map/psum | solution.py:65
  9.5 10.0 %collective-permute-start = (bf16[2,512,256]{2,1,0:T(8,128)(2,1)}, bf16[2,512,256]{2,1,0:T(8,128)(2,1)S(1)}, u32[]{:S(2)}, u32[]{:S(2)}) collective-permute-start(bf16[2,512,256]{2,1,0:T(8,128)(2,1)} %get-tuple-element.46), channel_id=1, source_target_pairs={{0,1},{1,2},{2,3},{3,4},{4,5},{5,6},{6,7},{7,8},{8,9},{9,10},{10,1... | collective-permute-start | bytes 1572872 | tf_op jit(solution)/shard_map/ppermute | solution.py:18
  11.8 8.4 %collective-permute-start.1 = (bf16[2,512,256]{2,1,0:T(8,128)(2,1)S(1)}, bf16[2,512,256]{2,1,0:T(8,128)(2,1)}, u32[]{:S(2)}, u32[]{:S(2)}) collective-permute-start(bf16[2,512,256]{2,1,0:T(8,128)(2,1)S(1)} %get-tuple-element.47), channel_id=1, source_target_pairs={{1,0},{2,1},{3,2},{4,3},{5,4},{6,5},{7,6},{8,7},{9,8},{10,9},{11,1... | collective-permute-start | bytes 1572872 | tf_op jit(solution)/shard_map/ppermute | solution.py:19
  15.7 4.6 %copy-start.3 = (bf16[2,2048,256]{2,1,0:T(8,128)(2,1)S(1)}, bf16[2,2048,256]{2,1,0:T(8,128)(2,1)}, u32[]{:S(2)}) copy-start(bf16[2,2048,256]{2,1,0:T(8,128)(2,1)} %param.12) | copy-start | bytes 6291460
  19.5 0.8 copy-start.13
  33.1 2.2 copy-start.8
  35.3 1.6 copy-start.11
  35.3 1.6 copy-start.15
  36.8 7.9 %copy-start.9 = (bf16[4096,256]{1,0:T(8,128)(2,1)}, bf16[4096,256]{1,0:T(8,128)(2,1)S(1)}, u32[]{:S(2)}) copy-start(bf16[4096,256]{1,0:T(8,128)(2,1)S(1)} %get-tuple-element.48) | copy-start | bytes 6291460
  38.7 3.9 %copy-start.6 = (bf16[4096,256]{1,0:T(8,128)(2,1)}, bf16[4096,256]{1,0:T(8,128)(2,1)S(1)}, u32[]{:S(2)}) copy-start(bf16[4096,256]{1,0:T(8,128)(2,1)S(1)} %fusion.8) | copy-start | bytes 6291460
  38.7 2.4 %copy-start.4 = (bf16[2,2048,256]{2,1,0:T(8,128)(2,1)S(1)}, bf16[2,2048,256]{2,1,0:T(8,128)(2,1)}, u32[]{:S(2)}) copy-start(bf16[2,2048,256]{2,1,0:T(8,128)(2,1)} %param.12) | copy-start | bytes 6291460
  97.4 12.1 %copy-start.10 = (bf16[4096,256]{1,0:T(8,128)(2,1)S(1)}, bf16[4096,256]{1,0:T(8,128)(2,1)}, u32[]{:S(2)}) copy-start(bf16[4096,256]{1,0:T(8,128)(2,1)} %copy-done.9) | copy-start | bytes 6291460
  100.3 12.8 %copy-start.5 = (f32[2,24,128,256]{3,1,2,0:T(8,128)S(1)}, f32[2,24,128,256]{3,1,2,0:T(8,128)}, u32[]{:S(2)}) copy-start(f32[2,24,128,256]{3,1,2,0:T(8,128)} %get-tuple-element.51) | copy-start | bytes 18874372
  100.3 102.7 %collective-permute-start.2 = (bf16[2,4,128,256]{3,1,2,0:T(4,128)(2,1)}, bf16[2,4,128,256]{3,1,2,0:T(4,128)(2,1)S(1)}, u32[]{:S(2)}, u32[]{:S(2)}) collective-permute-start(bf16[2,4,128,256]{3,1,2,0:T(4,128)(2,1)} %get-tuple-element.45), channel_id=1, source_target_pairs={{0,1},{1,2},{2,3},{3,4},{4,5},{5,6},{6,7},{7,8},{8,9},{9,10},{10,1... | collective-permute-start | bytes 1572872 | tf_op jit(solution)/shard_map/ppermute | solution.py:27
  111.6 94.4 %collective-permute-start.3 = (bf16[2,4,128,256]{3,1,2,0:T(4,128)(2,1)S(1)}, bf16[2,4,128,256]{3,1,2,0:T(4,128)(2,1)S(1)}, u32[]{:S(2)}, u32[]{:S(2)}) collective-permute-start(bf16[2,4,128,256]{3,1,2,0:T(4,128)(2,1)S(1)} %get-tuple-element.44), channel_id=1, source_target_pairs={{1,0},{2,1},{3,2},{4,3},{5,4},{6,5},{7,6},{8,7},{9,8},{10,9},{11,1... | collective-permute-start | bytes 1572872 | tf_op jit(solution)/shard_map/ppermute | solution.py:27
  209.0 4.8 %copy-start.7 = (bf16[4096,256]{1,0:T(8,128)(2,1)S(1)}, bf16[4096,256]{1,0:T(8,128)(2,1)}, u32[]{:S(2)}) copy-start(bf16[4096,256]{1,0:T(8,128)(2,1)} %copy-done.6) | copy-start | bytes 6291460
  209.0 4.8 %copy-start.12 = (bf16[2,2048,256]{2,1,0:T(8,128)(2,1)S(1)}, bf16[2,2048,256]{2,1,0:T(8,128)(2,1)}, u32[]{:S(2)}) copy-start(bf16[2,2048,256]{2,1,0:T(8,128)(2,1)} %param.13) | copy-start | bytes 6291460
  209.0 4.8 %copy-start.14 = (bf16[256,256]{1,0:T(8,128)(2,1)S(1)}, bf16[256,256]{1,0:T(8,128)(2,1)}, u32[]{:S(2)}) copy-start(bf16[256,256]{1,0:T(8,128)(2,1)} %param.17) | copy-start | bytes 393220
  209.0 7.1 %copy-start.1 = (bf16[256,256]{1,0:T(8,128)(2,1)S(1)}, bf16[256,256]{1,0:T(8,128)(2,1)}, u32[]{:S(2)}) copy-start(bf16[256,256]{1,0:T(8,128)(2,1)} %param.18) | copy-start | bytes 393220
Sparse Core Ops, SparseCore 0:
  97.5 100.9 all-reduce.2
where the time goes:
time: 224 us; the launch traced here: 223 us
  waiting for transfers between devices  82.9 us (37%)
  matrix products  57.2 us (26%)
  local copies, waits for them, and re-layouts  42.8 us (19%)
  starting transfers between devices  14.4 us (6%)
  between operations  14.3 us (6%)
  other arithmetic  11.4 us (5%)
    psum x1, waiting for transfers between devices, body(): lax.psum((jnp.dot(activated.T, flat_cot, preferred_element_type=jnp.float...  82.9 us
    dot_general x1, matrix products, fold_rows(): jnp.einsum('ms,cmjf->csjf', one_hot, contrib_rows, precision=lax.Precisio...  22.7 us
    transpose x1, local copies, waits for them, and re-layouts, body(): jnp.einsum('rkij,crif->crkjf', live_tiles, d_blocks, preferred_element_ty...  18 us
    ppermute x2, starting transfers between devices, shifted(): lax.ppermute(value, axis, [(source, source + steps) for source in range(f...  10.7 us
    dot_general x1, matrix products, body(): jnp.einsum('rkij,crif->crkjf', live_tiles, d_blocks, preferred_element_ty...  10.4 us
    unnamed x35, local copies, waits for them, and re-layouts  6.27 us
    dot_general x1, matrix products, body(): jnp.einsum('rkij,crkjf->crif', live_tiles, picked, preferred_element_type...  5.91 us
    gather x1, local copies, waits for them, and re-layouts, body(): picked = jnp.take(ext_blocks, local_index, axis=1)  5.6 us
  transfers between devices with their start and end apart: 5, of which 1 were waited for; matrix products, arithmetic and copies ran while one was open for 10% of the time, Pallas kernels for 0%

commit v1 on v0

v1 whole, which is shorter than its diff:
```python
import functools
import math

import jax
import jax.numpy as jnp
from jax import lax
from jax.experimental import pallas as pl
from jax.experimental.pallas import tpu as pltpu
from jax.sharding import PartitionSpec as P

R = 4
F32 = jnp.float32
BF16 = jnp.bfloat16
ANY = pl.BlockSpec(memory_space=pl.ANY)
VM = pl.BlockSpec(memory_space=pltpu.VMEM)
SM = pl.BlockSpec(memory_space=pltpu.SMEM)
PARAMS = pltpu.CompilerParams(vmem_limit_bytes=56 * 1024 * 1024)


def mm(a, b):
    return lax.dot_general(a, b, (((1,), (0,)), ((), ())), preferred_element_type=F32)


def mm_bt(a, b):
    return lax.dot_general(a, b, (((1,), (1,)), ((), ())), preferred_element_type=F32)


def mm_at(a, b):
    return lax.dot_general(a, b, (((0,), (0,)), ((), ())), preferred_element_type=F32)


def block_at(index, size):
    return pl.ds(pl.multiple_of(index * size, size), size)


def start_all(copies):
    for copy in copies:
        copy.start()
    return copies


def wait_all(copies):
    for copy in copies:
        copy.wait()


def load_row(a_ref, row, live, slots):
    return jnp.concatenate(
        [jnp.where(k < live, a_ref[row, k], jnp.zeros((), BF16)) for k in range(slots)], axis=1
    )


def aggregate_rows(a_ref, acat_ref, agg_ref, x_ref, cols, live, slots, size):
    clones = x_ref.shape[0]
    for r in range(R):
        acat = load_row(a_ref, r, live(r), slots)
        acat_ref[r] = acat
        for c in range(clones):
            picked = jnp.concatenate(
                [x_ref[c, block_at(cols(r, k), size), :] for k in range(slots)], axis=0
            )
            agg_ref[c, r * size : (r + 1) * size, :] = mm(acat, picked).astype(BF16)


def dense_forward(x, agg, cot, ws, wn, wo):
    pre = mm(x, ws) + mm(agg, wn)
    sigma = jax.nn.sigmoid(pre)
    act = (pre * sigma).astype(BF16)
    d_pre = (mm_bt(cot, wo) * sigma * (1.0 + pre * (1.0 - sigma))).astype(BF16)
    return act, d_pre


def main_kernel(
    idx, cols_ref, cnt_ref, x_hbm, nh_hbm, a_hbm, cot_hbm, ws, wn, wo,
    upd_hbm, acc_hbm, nmsg_hbm, g_hbm,
    xe, a_s, cot_s, acc, upd_s, nmsg_s, g_s, acat_s, agg_s, da_s, sems,
):
    clones, rows, hidden = x_hbm.shape
    per, slots, size, _ = a_hbm.shape
    width = R * size
    chunks = per // R - 1
    odd = lax.rem(idx[0], 2)
    first = idx[0] * per - R
    off = jnp.where(odd == 1, 0, R)
    near = jnp.where(odd == 1, 0, R + per)
    ins = start_all(
        [
            pltpu.make_async_copy(x_hbm, xe.at[:, pl.ds(width, rows), :], sems.at[0]),
            pltpu.make_async_copy(
                nh_hbm, xe.at[:, pl.ds(pl.multiple_of(near * size, width), width), :], sems.at[1]
            ),
        ]
    )
    a_in, cot_in = [], []
    for i in range(chunks):
        a_in += start_all(
            [pltpu.make_async_copy(a_hbm.at[pl.ds(off + R * i, R)], a_s.at[i], sems.at[2 + i])]
        )
        start = pl.multiple_of((off + R * i) * size, width)
        cot_in += start_all(
            [
                pltpu.make_async_copy(
                    cot_hbm.at[:, pl.ds(start, width), :], cot_s.at[i], sems.at[2 + chunks + i]
                )
            ]
        )
    acc[...] = jnp.zeros_like(acc)
    outs = []
    wait_all(ins)
    for i in range(chunks):
        a_in[i].wait()
        base = off + R * i
        start = pl.multiple_of(base * size, width)

        def cols(r, k):
            return cols_ref[base + r, k] - first

        aggregate_rows(
            a_s.at[i], acat_s, agg_s, xe, cols, lambda r: cnt_ref[base + r], slots, size
        )
        cot_in[i].wait()
        for c in range(clones):
            x = xe[c, pl.ds(start + width, width), :]
            agg = agg_s[c]
            cot = cot_s[i, c]
            act, d_pre = dense_forward(x, agg, cot, ws[...], wn[...], wo[...])
            upd_s[i, c] = (x.astype(F32) + mm(act, wo[...])).astype(BF16)
            parts = (mm_at(x, d_pre), mm_at(agg, d_pre), mm_at(act, cot))
            for p, part in enumerate(parts):
                sl = slice(p * hidden, (p + 1) * hidden)
                if i == 0 and c == 0:
                    g_s[sl, :] = part
                else:
                    g_s[sl, :] += part
            da_s[:, c * hidden : (c + 1) * hidden] = mm_bt(d_pre, wn[...]).astype(BF16)
            acc[c, pl.ds(start + width, width), :] += cot.astype(F32) + mm_bt(d_pre, ws[...])
        outs += start_all(
            [
                pltpu.make_async_copy(
                    upd_s.at[i], upd_hbm.at[:, pl.ds(start, width), :], sems.at[2 + 2 * chunks + i]
                )
            ]
        )
        for r in range(R):
            msg = mm_at(acat_s[r], da_s[r * size : (r + 1) * size, :])
            for k in range(slots):
                for c in range(clones):
                    at = block_at(cols(r, k), size)
                    acc[c, at, :] += msg[k * size : (k + 1) * size, c * hidden : (c + 1) * hidden]
    nmsg_s[...] = acc[:, pl.ds(pl.multiple_of(near * size, width), width), :].astype(BF16)
    last = 2 + 3 * chunks
    outs += start_all(
        [
            pltpu.make_async_copy(nmsg_s, nmsg_hbm, sems.at[last]),
            pltpu.make_async_copy(g_s, g_hbm, sems.at[last + 1]),
            pltpu.make_async_copy(acc.at[:, pl.ds(width, rows), :], acc_hbm, sems.at[last + 2]),
        ]
    )
    wait_all(outs)


def far_kernel(
    idx, cols_ref, cnt_ref, x_hbm, fh_hbm, a_hbm, cot_hbm, g_hbm, ws, wn, wo,
    fmsg_ref, keep_ref, send_ref, act_ref, dpre_ref, da_ref,
    xw, a_s, cot_s, g_s, fm_s, acat_s, agg_s, sems,
):
    clones, rows, hidden = x_hbm.shape
    per, slots, size, _ = a_hbm.shape
    width = R * size
    odd = lax.rem(idx[0], 2)
    first = idx[0] * per
    base = jnp.where(odd == 1, per - R, 0)
    start = pl.multiple_of(base * size, width)
    window = first + jnp.where(odd == 1, per - 2 * R, -R)
    halo_at = pl.multiple_of(jnp.where(odd == 1, 2 * width, 0), width)
    local_at = pl.multiple_of(jnp.where(odd == 1, 0, width), width)
    local_from = pl.multiple_of(jnp.where(odd == 1, rows - 2 * width, 0), width)
    ins = start_all(
        [
            pltpu.make_async_copy(fh_hbm, xw.at[:, pl.ds(halo_at, width), :], sems.at[0]),
            pltpu.make_async_copy(
                x_hbm.at[:, pl.ds(local_from, 2 * width), :],
                xw.at[:, pl.ds(local_at, 2 * width), :],
                sems.at[1],
            ),
            pltpu.make_async_copy(a_hbm.at[pl.ds(base, R)], a_s, sems.at[2]),
            pltpu.make_async_copy(cot_hbm.at[:, pl.ds(start, width), :], cot_s, sems.at[3]),
            pltpu.make_async_copy(g_hbm, g_s, sems.at[4]),
        ]
    )
    fm_s[...] = jnp.zeros_like(fm_s)
    wait_all(ins)

    def cols(r, k):
        return cols_ref[base + r, k] - window

    aggregate_rows(a_s, acat_s, agg_s, xw, cols, lambda r: cnt_ref[base + r], slots, size)
    mine = pl.multiple_of(jnp.where(odd == 1, width, width), width)
    for c in range(clones):
        x = xw[c, pl.ds(mine, width), :]
        agg = agg_s[c]
        cot = cot_s[c]
        act, d_pre = dense_forward(x, agg, cot, ws[...], wn[...], wo[...])
        act_ref[c] = act
        dpre_ref[c] = d_pre
        da_ref[:, c * hidden : (c + 1) * hidden] = mm_bt(d_pre, wn[...]).astype(BF16)
        parts = (mm_at(x, d_pre), mm_at(agg, d_pre), mm_at(act, cot))
        for p, part in enumerate(parts):
            g_s[p * hidden : (p + 1) * hidden, :] += part
    halo_block = jnp.where(odd == 1, 2 * R, 0)
    for r in range(R):
        for k in range(slots):
            target = cols(r, k) - halo_block

            @pl.when((k < cnt_ref[base + r]) & (target >= 0) & (target < R))
            def _():
                msg = mm_at(a_s[r, k], da_ref[r * size : (r + 1) * size, :])
                for c in range(clones):
                    fm_s[c, block_at(target, size), :] += msg[:, c * hidden : (c + 1) * hidden]

    fmsg_ref[...] = fm_s[...].astype(BF16)
    half = g_s.shape[0] // 2
    keep_ref[...] = g_s[pl.ds(pl.multiple_of(odd * half, half), half), :]
    send_ref[...] = g_s[pl.ds(pl.multiple_of((1 - odd) * half, half), half), :]


def last_kernel(
    idx, cols_ref, cnt_ref, x_hbm, a_hbm, cot_hbm, acc_hbm, nrecv_hbm, frecv_hbm, act_hbm, dpre_hbm, da_hbm,
    ws, wo, upd_in, upd_hbm, grad_hbm,
    acc, a_s, x_s, cot_s, near_s, far_s, act_s, dpre_s, da_s, upd_s, grad_s, sems,
):
    clones, rows, hidden = x_hbm.shape
    per, slots, size, _ = a_hbm.shape
    width = R * size
    odd = lax.rem(idx[0], 2)
    first = idx[0] * per
    base = jnp.where(odd == 1, per - R, 0)
    start = pl.multiple_of(base * size, width)
    near_start = pl.multiple_of(jnp.where(odd == 1, 0, rows - width), width)
    pairs = (
        (a_hbm.at[pl.ds(base, R)], a_s),
        (x_hbm.at[:, pl.ds(start, width), :], x_s),
        (cot_hbm.at[:, pl.ds(start, width), :], cot_s),
        (act_hbm, act_s),
        (dpre_hbm, dpre_s),
        (da_hbm, da_s),
        (acc_hbm, acc),
        (nrecv_hbm, near_s),
        (frecv_hbm, far_s),
    )
    ins = start_all([pltpu.make_async_copy(s, d, sems.at[j]) for j, (s, d) in enumerate(pairs)])
    wait_all(ins)
    for c in range(clones):
        upd_s[c] = (x_s[c].astype(F32) + mm(act_s[c], wo[...])).astype(BF16)
    store = pltpu.make_async_copy(upd_s, upd_hbm.at[:, pl.ds(start, width), :], sems.at[len(pairs)])
    store.start()
    for c in range(clones):
        acc[c, pl.ds(start, width), :] += (
            cot_s[c].astype(F32) + mm_bt(dpre_s[c], ws[...]) + far_s[c].astype(F32)
        )
        acc[c, pl.ds(near_start, width), :] += near_s[c].astype(F32)
    for r in range(R):
        for k in range(slots):
            target = cols_ref[base + r, k] - first

            @pl.when((k < cnt_ref[base + r]) & (target >= 0) & (target < per))
            def _():
                msg = mm_at(a_s[r, k], da_s[r * size : (r + 1) * size, :])
                for c in range(clones):
                    acc[c, block_at(target, size), :] += msg[:, c * hidden : (c + 1) * hidden]

    grad_s[...] = acc[...].astype(BF16)
    out = pltpu.make_async_copy(grad_s, grad_hbm, sems.at[len(pairs) + 1])
    out.start()
    store.wait()
    out.wait()


def swap(value, bit):
    count = lax.axis_size("dom")
    return lax.ppermute(value, "dom", [(i, i ^ bit) for i in range(count)])


def halves(value, high):
    half = value.shape[0] // 2
    low_part, high_part = value[:half], value[half:]
    return jnp.where(high, high_part, low_part), jnp.where(high, low_part, high_part)


def join(mine, other, high):
    return jnp.where(
        high, jnp.concatenate([other, mine], axis=0), jnp.concatenate([mine, other], axis=0)
    )


def reduce_all(keep, send, index, factor):
    count = lax.axis_size("dom")
    total = keep + swap(send, 1)
    bits = [1 << b for b in range(1, count.bit_length() - 1)]
    scatter = bits[-2:] if len(bits) > 2 else []
    for bit in scatter:
        mine, other = halves(total, (index & bit) != 0)
        total = mine + swap(other.astype(BF16), bit).astype(F32)
    for bit in bits:
        if bit not in scatter:
            rounded = total.astype(BF16)
            total = rounded.astype(F32) + swap(rounded, bit).astype(F32)
    result = total.astype(BF16)
    for bit in reversed(scatter):
        result = join(result, swap(result, bit), (index & bit) != 0)
    result = join(result, swap(result, 1), (index & 1) != 0)
    return result.astype(F32) * factor


def body(features, cotangent, adjacency, tile_cols, tile_counts, w_self, w_neigh, w_out):
    clones, rows, hidden = features.shape
    per, slots, size, _ = adjacency.shape
    width = R * size
    count = lax.axis_size("dom")
    index = lax.axis_index("dom")
    odd = (index & 1) == 1
    idx = index.reshape(1).astype(jnp.int32)
    near_pairs = [(i, i ^ 1) for i in range(count)]
    far_pairs = [(i, ((i + 1) ^ 1) - 1) for i in range(1, count - 1)]
    far_start = jnp.where(odd, rows - width, 0)
    near_start = jnp.where(odd, 0, rows - width)
    far_out = lax.dynamic_slice_in_dim(features, far_start, width, axis=1)
    near_out = lax.dynamic_slice_in_dim(features, near_start, width, axis=1)
    far_halo = lax.ppermute(far_out, "dom", far_pairs)
    near_halo = lax.ppermute(near_out, "dom", near_pairs)

    sds = jax.ShapeDtypeStruct
    chunks = per // R - 1
    upd, acc, near_msg, g = pl.pallas_call(
        main_kernel,
        out_shape=(
            sds((clones, rows, hidden), BF16),
            sds((clones, rows, hidden), F32),
            sds((clones, width, hidden), BF16),
            sds((3 * hidden, hidden), F32),
        ),
        in_specs=[SM, SM, SM, ANY, ANY, ANY, ANY, VM, VM, VM],
        out_specs=(ANY, ANY, ANY, ANY),
        scratch_shapes=[
            pltpu.VMEM((clones, rows + 2 * width, hidden), BF16),
            pltpu.VMEM((chunks, R, slots, size, size), BF16),
            pltpu.VMEM((chunks, clones, width, hidden), BF16),
            pltpu.VMEM((clones, rows + 2 * width, hidden), F32),
            pltpu.VMEM((chunks, clones, width, hidden), BF16),
            pltpu.VMEM((clones, width, hidden), BF16),
            pltpu.VMEM((3 * hidden, hidden), F32),
            pltpu.VMEM((R, size, slots * size), BF16),
            pltpu.VMEM((clones, width, hidden), BF16),
            pltpu.VMEM((width, clones * hidden), BF16),
            pltpu.SemaphoreType.DMA((5 + 3 * chunks,)),
        ],
        compiler_params=PARAMS,
        name="near_rows",
    )(idx, tile_cols, tile_counts, features, near_halo, adjacency, cotangent, w_self, w_neigh, w_out)
    near_recv = lax.ppermute(near_msg, "dom", near_pairs)

    far_msg, keep, send, act, d_pre, d_agg = pl.pallas_call(
        far_kernel,
        out_shape=(
            sds((clones, width, hidden), BF16),
            sds((3 * hidden // 2, hidden), F32),
            sds((3 * hidden // 2, hidden), F32),
            sds((clones, width, hidden), BF16),
            sds((clones, width, hidden), BF16),
            sds((width, clones * hidden), BF16),
        ),
        in_specs=[SM, SM, SM, ANY, ANY, ANY, ANY, ANY, VM, VM, VM],
        out_specs=(VM,) * 6,
        scratch_shapes=[
            pltpu.VMEM((clones, 3 * width, hidden), BF16),
            pltpu.VMEM((R, slots, size, size), BF16),
            pltpu.VMEM((clones, width, hidden), BF16),
            pltpu.VMEM((3 * hidden, hidden), F32),
            pltpu.VMEM((clones, width, hidden), F32),
            pltpu.VMEM((R, size, slots * size), BF16),
            pltpu.VMEM((clones, width, hidden), BF16),
            pltpu.SemaphoreType.DMA((5,)),
        ],
        compiler_params=PARAMS,
        name="far_rows",
    )(idx, tile_cols, tile_counts, features, far_halo, adjacency, cotangent, g, w_self, w_neigh, w_out)
    far_recv = lax.ppermute(far_msg, "dom", far_pairs)

    factor = 1.0 / math.sqrt(2.0 * rows * count)
    sums = reduce_all(keep, send, index, factor)

    updated, grad_features = pl.pallas_call(
        last_kernel,
        out_shape=(sds((clones, rows, hidden), BF16), sds((clones, rows, hidden), BF16)),
        in_specs=[SM, SM, SM] + [ANY] * 9 + [VM, VM, ANY],
        out_specs=(ANY, ANY),
        input_output_aliases={14: 0},
        scratch_shapes=[
            pltpu.VMEM((clones, rows, hidden), F32),
            pltpu.VMEM((R, slots, size, size), BF16),
            pltpu.VMEM((clones, width, hidden), BF16),
            pltpu.VMEM((clones, width, hidden), BF16),
            pltpu.VMEM((clones, width, hidden), BF16),
            pltpu.VMEM((clones, width, hidden), BF16),
            pltpu.VMEM((clones, width, hidden), BF16),
            pltpu.VMEM((clones, width, hidden), BF16),
            pltpu.VMEM((width, clones * hidden), BF16),
            pltpu.VMEM((clones, width, hidden), BF16),
            pltpu.VMEM((clones, rows, hidden), BF16),
            pltpu.SemaphoreType.DMA((11,)),
        ],
        compiler_params=PARAMS,
        name="last_rows",
    )(
        idx, tile_cols, tile_counts, features, adjacency, cotangent, acc, near_recv, far_recv,
        act, d_pre, d_agg, w_self, w_out, upd,
    )
    return (
        updated,
        grad_features,
        sums[:hidden],
        sums[hidden : 2 * hidden],
        sums[2 * hidden :],
    )


def solution(mesh):
    return jax.shard_map(
        body,
        mesh=mesh,
        in_specs=(
            P("groups", "dom", None),
            P("groups", "dom", None),
            P("dom", None, None, None),
            P("dom", None),
            P("dom"),
            P(),
            P(),
            P(),
        ),
        out_specs=(
            P("groups", "dom", None),
            P("groups", "dom", None),
            P("groups", None),
            P("groups", None),
            P("groups", None),
        ),
        check_vma=False,
    )
```

time: 224 us -> 77.1 us (0.34)
  waiting for transfers between devices: 82.9 us -> 21.4 us
  matrix products: 57.2 us -> 0 us
  local copies, waits for them, and re-layouts: 42.8 us -> 5.39 us
  Pallas kernels: 0 us -> 30.2 us
  between operations: 14.3 us -> 0.84 us
  other arithmetic: 11.4 us -> 1.33 us
  starting transfers between devices: 14.4 us -> 17.3 us
    psum x1 -> x0, waiting for transfers between devices: 82.9 us -> none  [body(): lax.psum((jnp.dot(activated.T, flat_cot, preferred_element_type=jnp.float...]
    dot_general x12 -> x0, matrix products: 57.2 us -> none  [the longest x1 22.7 us: fold_rows(): jnp.einsum('ms,cmjf->csjf', one_hot, contrib_rows, precision=lax.Precisio...]
    pallas_call x0 -> x3, Pallas kernels: none -> 30.2 us  [the longest x1 13.5 us: body(): pl.pallas_call(main_kernel, out_shape=(sds((clones, rows, hidden), BF16),...]
    ppermute x4 -> x11, waiting for transfers between devices: 0.01 us -> 21.4 us  [the longest x7 21.2 us: swap(): return lax.ppermute(value, 'dom', [(i, i ^ bit) for i in range(count)])]
    transpose x1 -> x0, local copies, waits for them, and re-layouts: 18 us -> none  [body(): jnp.einsum('rkij,crif->crkjf', live_tiles, d_blocks, preferred_element_ty...]
    slice x3 -> x1, local copies, waits for them, and re-layouts: 7.61 us -> 0.89 us  [body(): sums[2 * hidden:]]
    scatter-add x2 -> x0, other arithmetic: 5.91 us -> none  [the longest x1 2.96 us: body(): center = center.at[:, :R].add(from_below.astype(jnp.float32))]
    gather x1 -> x0, local copies, waits for them, and re-layouts: 5.6 us -> none  [body(): picked = jnp.take(ext_blocks, local_index, axis=1)]
  transfers between devices with their start and end apart: 5 -> 11, of which waited for: 1 -> 7; matrix products, arithmetic and copies ran while one was open for 10% -> 1% of each run, Pallas kernels for 0% -> 31%
where the time goes in v1:
time: 77.1 us; the launch traced here: 76.5 us
  Pallas kernels  30.2 us (39%)
  waiting for transfers between devices  21.4 us (28%)
  starting transfers between devices  17.3 us (22%)
  local copies, waits for them, and re-layouts  5.39 us (7%)
  other arithmetic  1.33 us (2%)
  between operations  0.84 us (1%)
    ppermute x7, waiting for transfers between devices, swap(): return lax.ppermute(value, 'dom', [(i, i ^ bit) for i in range(count)])  21.2 us
    ppermute x7, starting transfers between devices, swap(): return lax.ppermute(value, 'dom', [(i, i ^ bit) for i in range(count)])  15.4 us
    pallas_call x1, Pallas kernels, body(): pl.pallas_call(main_kernel, out_shape=(sds((clones, rows, hidden), BF16),...  13.5 us
    pallas_call x1, Pallas kernels, body(): pl.pallas_call(last_kernel, out_shape=(sds((clones, rows, hidden), BF16),...  9.96 us
    pallas_call x1, Pallas kernels, body(): pl.pallas_call(far_kernel, out_shape=(sds((clones, width, hidden), BF16),...  6.76 us
    unnamed x15, local copies, waits for them, and re-layouts  3.22 us
  transfers between devices with their start and end apart: 11, of which 7 were waited for; matrix products, arithmetic and copies ran while one was open for 1% of the time, Pallas kernels for 31%

profile of v1, /device:TPU:0, one launch (start us, length us, event | category | flops | bytes accessed | tf_op | source)
XLA Modules:
  0.0 76.5 jit_solution(3743610433692688035)
XLA Ops:
  0.7 1.3 %constant_dynamic-slice_fusion = (bf16[2,512,256]{2,1,0:T(8,128)(2,1)S(1)}, bf16[2,512,256]{2,1,0:T(8,128)(2,1)S(1)}) fusion(bf16[2,2048,256]{2,1,0:T(8,128)(2,1)} %x_hbm.5, s32[]{:T(128)S(6)} %select_n.58, s32[]{:T(128)S(6)} %select_n.57), kind=kLoop, calls=%fused_computation.9 | loop fusion | bytes 2097160 | tf_op jit(solution)/shard_map/dynamic_slice | solution.py:327
  2.5 0.7 collective-permute-start.2
  3.2 0.7 copy.16.cols_ref
  4.0 0.8 %copy-done.3 = bf16[2,512,256]{2,1,0:T(8,128)(2,1)} copy-done((bf16[2,512,256]{2,1,0:T(8,128)(2,1)}, bf16[2,512,256]{2,1,0:T(8,128)(2,1)S(1)}, u32[]{:S(2)}) %copy-start.3) | copy-done | bytes 524312
  4.8 13.5 %near_rows.1 = (bf16[2,2048,256]{2,1,0:T(8,128)(2,1)}, f32[2,2048,256]{2,1,0:T(8,128)}, bf16[2,512,256]{2,1,0:T(8,128)(2,1)}, f32[768,256]{1,0:T(8,128)}) custom-call(s32[1]{0:T(128)} %bitcast.idx, s32[16,4]{1,0:T(8,128)} %copy.16.cols_ref, s32[16]{0:T(128)} %cnt_ref.5, bf16[2,2048,256]{2,1,0:T(8,128)(2,1)} %x_hbm.5, bf16[2,512,256]{2,1,0:T(8,128)(2,1)} %copy-done.3, ...), custom_call_target="tpu_custom_call" | custom-call | tf_op jit(solution)/shard_map/near_rows/pallas_call | solution.py:334
  18.3 0.8 %copy-done.2 = bf16[2,512,256]{2,1,0:T(8,128)(2,1)} copy-done((bf16[2,512,256]{2,1,0:T(8,128)(2,1)}, bf16[2,512,256]{2,1,0:T(8,128)(2,1)S(1)}, u32[]{:S(2)}) %copy-start.2) | copy-done | bytes 524312
  19.1 6.8 %far_rows.1 = (bf16[2,512,256]{2,1,0:T(8,128)(2,1)}, f32[384,256]{1,0:T(8,128)}, f32[384,256]{1,0:T(8,128)}, bf16[2,512,256]{2,1,0:T(8,128)(2,1)}, bf16[2,512,25...) custom-call(s32[1]{0:T(128)} %bitcast.idx, s32[16,4]{1,0:T(8,128)} %copy.16.cols_ref, s32[16]{0:T(128)} %cnt_ref.5, ...), custom_call_target="tpu_custom_call" | custom-call | tf_op jit(solution)/shard_map/far_rows/pallas_call | solution.py:362
  25.9 4.4 %collective-permute-start.4 = (f32[384,256]{1,0:T(8,128)}, f32[384,256]{1,0:T(8,128)S(1)}, u32[]{:S(2)}, u32[]{:S(2)}) collective-permute-start(f32[384,256]{1,0:T(8,128)} %get-tuple-element.28), channel_id=1, source_target_pairs={{0,1},{1,0},{2,3},{3,2},{4,5},{5,4},{6,7},{7,6},{8,9},{9,8},{10,11... | collective-permute-start | bytes 1179656 | tf_op jit(solution)/shard_map/ppermute | solution.py:281
  30.3 1.6 %collective-permute-done.4 = f32[384,256]{1,0:T(8,128)S(1)} collective-permute-done((f32[384,256]{1,0:T(8,128)}, f32[384,256]{1,0:T(8,128)S(1)}, u32[]{:S(2)}, u32[]{:S(2)}) %collective-permute-start.4) | collective-permute-done | bytes 393248 | tf_op jit(solution)/shard_map/ppermute | solution.py:281
  31.8 1.0 %add.14 = f32[384,256]{1,0:T(8,128)S(1)} add(f32[384,256]{1,0:T(8,128)} %get-tuple-element.27, f32[384,256]{1,0:T(8,128)S(1)} %collective-permute-done.4) | non-fusion elementwise | flops 98304 | bytes 1179648 | tf_op jit(solution)/shard_map/add | solution.py:298
  32.9 2.3 %collective-permute-start.5 = (bf16[192,256]{1,0:T(8,128)(2,1)S(1)}, bf16[192,256]{1,0:T(8,128)(2,1)S(1)}, u32[]{:S(2)}, u32[]{:S(2)}) collective-permute-start(bf16[192,256]{1,0:T(8,128)(2,1)S(1)} %select_convert_fusion), channel_id=1, source_target_pairs={{0,4},{1,5},{2,6},{3,7},{4,0},{5,1},{6,2},{7,3},{8,12},{9,13},{10,... | collective-permute-start | bytes 294920 | tf_op jit(solution)/shard_map/ppermute | solution.py:281
  35.2 3.3 %collective-permute-done.5 = bf16[192,256]{1,0:T(8,128)(2,1)S(1)} collective-permute-done((bf16[192,256]{1,0:T(8,128)(2,1)S(1)}, bf16[192,256]{1,0:T(8,128)(2,1)S(1)}, u32[]{:S(2)}, u32[]{:S(2)}) %collective-permute-start.5) | collective-permute-done | bytes 98336 | tf_op jit(solution)/shard_map/ppermute | solution.py:281
  38.5 2.6 %collective-permute-start.6 = (bf16[96,256]{1,0:T(8,128)(2,1)S(1)}, bf16[96,256]{1,0:T(8,128)(2,1)S(1)}, u32[]{:S(2)}, u32[]{:S(2)}) collective-permute-start(bf16[96,256]{1,0:T(8,128)(2,1)S(1)} %select_convert_fusion.1), channel_id=1, source_target_pairs={{0,8},{1,9},{2,10},{3,11},{4,12},{5,13},{6,14},{7,15},{8,0},{9,1},... | collective-permute-start | bytes 147464 | tf_op jit(solution)/shard_map/ppermute | solution.py:281
  41.2 2.7 %collective-permute-done.6 = bf16[96,256]{1,0:T(8,128)(2,1)S(1)} collective-permute-done((bf16[96,256]{1,0:T(8,128)(2,1)S(1)}, bf16[96,256]{1,0:T(8,128)(2,1)S(1)}, u32[]{:S(2)}, u32[]{:S(2)}) %collective-permute-start.6) | collective-permute-done | bytes 49184 | tf_op jit(solution)/shard_map/ppermute | solution.py:281
  43.9 1.4 %collective-permute-start.7 = (bf16[96,256]{1,0:T(8,128)(2,1)S(1)}, bf16[96,256]{1,0:T(8,128)(2,1)S(1)}, u32[]{:S(2)}, u32[]{:S(2)}) collective-permute-start(bf16[96,256]{1,0:T(8,128)(2,1)S(1)} %add_convert_fusion.1), channel_id=1, source_target_pairs={{0,2},{1,3},{2,0},{3,1},{4,6},{5,7},{6,4},{7,5},{8,10},{9,11},{10,... | collective-permute-start | bytes 147464 | tf_op jit(solution)/shard_map/ppermute | solution.py:281
  45.3 2.8 %collective-permute-done.7 = bf16[96,256]{1,0:T(8,128)(2,1)S(1)} collective-permute-done((bf16[96,256]{1,0:T(8,128)(2,1)S(1)}, bf16[96,256]{1,0:T(8,128)(2,1)S(1)}, u32[]{:S(2)}, u32[]{:S(2)}) %collective-permute-start.7) | collective-permute-done | bytes 49184 | tf_op jit(solution)/shard_map/ppermute | solution.py:281
  48.1 2.4 %collective-permute-start.8 = (bf16[96,256]{1,0:T(8,128)(2,1)S(1)}, bf16[96,256]{1,0:T(8,128)(2,1)S(1)}, u32[]{:S(2)}, u32[]{:S(2)}) collective-permute-start(bf16[96,256]{1,0:T(8,128)(2,1)S(1)} %add_convert_fusion), channel_id=1, source_target_pairs={{0,8},{1,9},{2,10},{3,11},{4,12},{5,13},{6,14},{7,15},{8,0},{9,1},... | collective-permute-start | bytes 147464 | tf_op jit(solution)/shard_map/ppermute | solution.py:281
  50.5 0.7 collective-permute-start.3
  51.2 1.9 %collective-permute-done.8 = bf16[96,256]{1,0:T(8,128)(2,1)S(1)} collective-permute-done((bf16[96,256]{1,0:T(8,128)(2,1)S(1)}, bf16[96,256]{1,0:T(8,128)(2,1)S(1)}, u32[]{:S(2)}, u32[]{:S(2)}) %collective-permute-start.8) | collective-permute-done | bytes 49184 | tf_op jit(solution)/shard_map/ppermute | solution.py:281
  53.2 2.3 %collective-permute-start.9 = (bf16[192,256]{1,0:T(8,128)(2,1)S(1)}, bf16[192,256]{1,0:T(8,128)(2,1)S(1)}, u32[]{:S(2)}, u32[]{:S(2)}) collective-permute-start(bf16[192,256]{1,0:T(8,128)(2,1)S(1)} %maximum_select_fusion.2), channel_id=1, source_target_pairs={{0,4},{1,5},{2,6},{3,7},{4,0},{5,1},{6,2},{7,3},{8,12},{9,13},{10,... | collective-permute-start | bytes 294920 | tf_op jit(solution)/shard_map/ppermute | solution.py:281
  55.4 8.9 %collective-permute-done.9 = bf16[192,256]{1,0:T(8,128)(2,1)S(1)} collective-permute-done((bf16[192,256]{1,0:T(8,128)(2,1)S(1)}, bf16[192,256]{1,0:T(8,128)(2,1)S(1)}, u32[]{:S(2)}, u32[]{:S(2)}) %collective-permute-start.9) | collective-permute-done | bytes 98336 | tf_op jit(solution)/shard_map/ppermute | solution.py:281
  64.5 0.8 %copy-done = bf16[2,512,256]{2,1,0:T(8,128)(2,1)} copy-done((bf16[2,512,256]{2,1,0:T(8,128)(2,1)}, bf16[2,512,256]{2,1,0:T(8,128)(2,1)S(1)}, u32[]{:S(2)}) %copy-start) | copy-done | bytes 524312
  65.5 10.0 %last_rows.1 = (bf16[2,2048,256]{2,1,0:T(8,128)(2,1)}, bf16[2,2048,256]{2,1,0:T(8,128)(2,1)}) custom-call(s32[1]{0:T(128)} %bitcast.idx, s32[16,4]{1,0:T(8,128)} %copy.16.cols_ref, s32[16]{0:T(128)} %cnt_ref.5, bf16[2,2048,256]{2,1,0:T(8,128)(2,1)} %x_hbm.5, bf16[16,4,128,128]{3,2,1,0:T(8,128)(2,1)} %a_hbm.5, ...), custom_call_target="tpu_custom_call", output_to_operand_aliasing={{0}: (14, {})} | custom-call | tf_op jit(solution)/shard_map/last_rows/pallas_call | solution.py:392
  75.6 0.9 %fusion = (f32[256,256]{1,0:T(8,128)}, f32[256,256]{1,0:T(8,128)}, f32[256,256]{1,0:T(8,128)}) fusion(f32[768,256]{1,0:T(8,128)S(1)} %convert_multiply_fusion), kind=kLoop, calls=%fused_computation.11 | loop fusion | bytes 1572864 | tf_op jit(solution)/shard_map/slice | solution.py:423
  (27 shorter events, 1.2 us)
Async XLA Ops:
  0.6 2.5 %copy-start.4 = (s32[16,4]{0,1:T(4,128)S(1)}, s32[16,4]{0,1:T(4,128)}, u32[]{:S(2)}) copy-start(s32[16,4]{0,1:T(4,128)} %param.11) | copy-start | bytes 772
  1.9 2.1 %collective-permute-start = (bf16[2,512,256]{2,1,0:T(8,128)(2,1)S(1)}, bf16[2,512,256]{2,1,0:T(8,128)(2,1)S(1)}, u32[]{:S(2)}, u32[]{:S(2)}) collective-permute-start(bf16[2,512,256]{2,1,0:T(8,128)(2,1)S(1)} %get-tuple-element.30), channel_id=1, source_target_pairs={{0,1},{1,0},{2,3},{3,2},{4,5},{5,4},{6,7},{7,6},{8,9},{9,8},{10,11... | collective-permute-start | bytes 1572872 | tf_op jit(solution)/shard_map/ppermute | solution.py:330
  2.5 15.9 %collective-permute-start.2 = (bf16[2,512,256]{2,1,0:T(8,128)(2,1)S(1)}, bf16[2,512,256]{2,1,0:T(8,128)(2,1)S(1)}, u32[]{:S(2)}, u32[]{:S(2)}) collective-permute-start(bf16[2,512,256]{2,1,0:T(8,128)(2,1)S(1)} %get-tuple-element.29), channel_id=1, source_target_pairs={{1,2},{2,1},{3,4},{4,3},{5,6},{6,5},{7,8},{8,7},{9,10},{10,9},{11,... | collective-permute-start | bytes 1572872 | tf_op jit(solution)/shard_map/ppermute | solution.py:329
  4.0 0.8 %copy-start.3 = (bf16[2,512,256]{2,1,0:T(8,128)(2,1)}, bf16[2,512,256]{2,1,0:T(8,128)(2,1)S(1)}, u32[]{:S(2)}) copy-start(bf16[2,512,256]{2,1,0:T(8,128)(2,1)S(1)} %collective-permute-done.nh_hbm) | copy-start | bytes 1572868
  18.3 0.8 %copy-start.2 = (bf16[2,512,256]{2,1,0:T(8,128)(2,1)}, bf16[2,512,256]{2,1,0:T(8,128)(2,1)S(1)}, u32[]{:S(2)}) copy-start(bf16[2,512,256]{2,1,0:T(8,128)(2,1)S(1)} %collective-permute-done.2.fh_hbm) | copy-start | bytes 1572868
  25.9 24.6 %copy-start.5 = (bf16[2,512,256]{2,1,0:T(8,128)(2,1)S(1)}, bf16[2,512,256]{2,1,0:T(8,128)(2,1)}, u32[]{:S(2)}) copy-start(bf16[2,512,256]{2,1,0:T(8,128)(2,1)} %get-tuple-element.18) | copy-start | bytes 1572868
  25.9 24.6 %copy-start.6 = (bf16[2,512,256]{2,1,0:T(8,128)(2,1)S(1)}, bf16[2,512,256]{2,1,0:T(8,128)(2,1)}, u32[]{:S(2)}) copy-start(bf16[2,512,256]{2,1,0:T(8,128)(2,1)} %get-tuple-element.20) | copy-start | bytes 1572868
  25.9 5.9 %collective-permute-start.4 = (f32[384,256]{1,0:T(8,128)}, f32[384,256]{1,0:T(8,128)S(1)}, u32[]{:S(2)}, u32[]{:S(2)}) collective-permute-start(f32[384,256]{1,0:T(8,128)} %get-tuple-element.28), channel_id=1, source_target_pairs={{0,1},{1,0},{2,3},{3,2},{4,5},{5,4},{6,7},{7,6},{8,9},{9,8},{10,11... | collective-permute-start | bytes 1179656 | tf_op jit(solution)/shard_map/ppermute | solution.py:281
  32.9 5.6 %collective-permute-start.5 = (bf16[192,256]{1,0:T(8,128)(2,1)S(1)}, bf16[192,256]{1,0:T(8,128)(2,1)S(1)}, u32[]{:S(2)}, u32[]{:S(2)}) collective-permute-start(bf16[192,256]{1,0:T(8,128)(2,1)S(1)} %select_convert_fusion), channel_id=1, source_target_pairs={{0,4},{1,5},{2,6},{3,7},{4,0},{5,1},{6,2},{7,3},{8,12},{9,13},{10,... | collective-permute-start | bytes 294920 | tf_op jit(solution)/shard_map/ppermute | solution.py:281
  38.5 5.3 %collective-permute-start.6 = (bf16[96,256]{1,0:T(8,128)(2,1)S(1)}, bf16[96,256]{1,0:T(8,128)(2,1)S(1)}, u32[]{:S(2)}, u32[]{:S(2)}) collective-permute-start(bf16[96,256]{1,0:T(8,128)(2,1)S(1)} %select_convert_fusion.1), channel_id=1, source_target_pairs={{0,8},{1,9},{2,10},{3,11},{4,12},{5,13},{6,14},{7,15},{8,0},{9,1},... | collective-permute-start | bytes 147464 | tf_op jit(solution)/shard_map/ppermute | solution.py:281
  43.9 4.2 %collective-permute-start.7 = (bf16[96,256]{1,0:T(8,128)(2,1)S(1)}, bf16[96,256]{1,0:T(8,128)(2,1)S(1)}, u32[]{:S(2)}, u32[]{:S(2)}) collective-permute-start(bf16[96,256]{1,0:T(8,128)(2,1)S(1)} %add_convert_fusion.1), channel_id=1, source_target_pairs={{0,2},{1,3},{2,0},{3,1},{4,6},{5,7},{6,4},{7,5},{8,10},{9,11},{10,... | collective-permute-start | bytes 147464 | tf_op jit(solution)/shard_map/ppermute | solution.py:281
  48.1 5.1 %collective-permute-start.8 = (bf16[96,256]{1,0:T(8,128)(2,1)S(1)}, bf16[96,256]{1,0:T(8,128)(2,1)S(1)}, u32[]{:S(2)}, u32[]{:S(2)}) collective-permute-start(bf16[96,256]{1,0:T(8,128)(2,1)S(1)} %add_convert_fusion), channel_id=1, source_target_pairs={{0,8},{1,9},{2,10},{3,11},{4,12},{5,13},{6,14},{7,15},{8,0},{9,1},... | collective-permute-start | bytes 147464 | tf_op jit(solution)/shard_map/ppermute | solution.py:281
  50.5 14.0 %collective-permute-start.1 = (bf16[2,512,256]{2,1,0:T(8,128)(2,1)S(1)}, bf16[2,512,256]{2,1,0:T(8,128)(2,1)S(1)}, u32[]{:S(2)}, u32[]{:S(2)}) collective-permute-start(bf16[2,512,256]{2,1,0:T(8,128)(2,1)S(1)} %copy-done.5), channel_id=1, source_target_pairs={{0,1},{1,0},{2,3},{3,2},{4,5},{5,4},{6,7},{7,6},{8,9},{9,8},{10,11... | collective-permute-start | bytes 1572872 | tf_op jit(solution)/shard_map/ppermute | solution.py:360
  50.5 14.0 %collective-permute-start.3 = (bf16[2,512,256]{2,1,0:T(8,128)(2,1)S(1)}, bf16[2,512,256]{2,1,0:T(8,128)(2,1)S(1)}, u32[]{:S(2)}, u32[]{:S(2)}) collective-permute-start(bf16[2,512,256]{2,1,0:T(8,128)(2,1)S(1)} %copy-done.6), channel_id=1, source_target_pairs={{1,2},{2,1},{3,4},{4,3},{5,6},{6,5},{7,8},{8,7},{9,10},{10,9},{11,... | collective-permute-start | bytes 1572872 | tf_op jit(solution)/shard_map/ppermute | solution.py:387
  53.2 11.2 %collective-permute-start.9 = (bf16[192,256]{1,0:T(8,128)(2,1)S(1)}, bf16[192,256]{1,0:T(8,128)(2,1)S(1)}, u32[]{:S(2)}, u32[]{:S(2)}) collective-permute-start(bf16[192,256]{1,0:T(8,128)(2,1)S(1)} %maximum_select_fusion.2), channel_id=1, source_target_pairs={{0,4},{1,5},{2,6},{3,7},{4,0},{5,1},{6,2},{7,3},{8,12},{9,13},{10,... | collective-permute-start | bytes 294920 | tf_op jit(solution)/shard_map/ppermute | solution.py:281
  64.4 11.0 %collective-permute-start.10 = (bf16[384,256]{1,0:T(8,128)(2,1)S(1)}, bf16[384,256]{1,0:T(8,128)(2,1)S(1)}, u32[]{:S(2)}, u32[]{:S(2)}) collective-permute-start(bf16[384,256]{1,0:T(8,128)(2,1)S(1)} %maximum_select_fusion.1), channel_id=1, source_target_pairs={{0,1},{1,0},{2,3},{3,2},{4,5},{5,4},{6,7},{7,6},{8,9},{9,8},{10,11... | collective-permute-start | bytes 589832 | tf_op jit(solution)/shard_map/ppermute | solution.py:281
  64.5 0.8 %copy-start = (bf16[2,512,256]{2,1,0:T(8,128)(2,1)}, bf16[2,512,256]{2,1,0:T(8,128)(2,1)S(1)}, u32[]{:S(2)}) copy-start(bf16[2,512,256]{2,1,0:T(8,128)(2,1)S(1)} %collective-permute-done.1.nrecv_hbm) | copy-start | bytes 1572868
  64.5 1.0 %copy-start.1 = (bf16[2,512,256]{2,1,0:T(8,128)(2,1)}, bf16[2,512,256]{2,1,0:T(8,128)(2,1)S(1)}, u32[]{:S(2)}) copy-start(bf16[2,512,256]{2,1,0:T(8,128)(2,1)S(1)} %collective-permute-done.3.frecv_hbm) | copy-start | bytes 1572868

commit v2 on v0

v2 whole, which is shorter than its diff:
```python
import functools
import math

import jax
import jax.numpy as jnp
from jax import lax
from jax.experimental import pallas as pl
from jax.experimental.pallas import tpu as pltpu
from jax.sharding import PartitionSpec as P

R = 4
F32 = jnp.float32
BF16 = jnp.bfloat16
ANY = pl.BlockSpec(memory_space=pltpu.HBM)
VM = pl.BlockSpec(memory_space=pltpu.VMEM)
SM = pl.BlockSpec(memory_space=pltpu.SMEM)
OWN_AT, EDGE_AT = 2, 3
COSTS = dict(mid_rows=1, near_rows=1, far_rows=1, messages=1, own_rows=1, edge_rows=1)
LIMIT = 12 * 1024 * 1024


def mm(a, b):
    return lax.dot_general(a, b, (((1,), (0,)), ((), ())), preferred_element_type=F32)


def mm_bt(a, b):
    return lax.dot_general(a, b, (((1,), (1,)), ((), ())), preferred_element_type=F32)


def mm_at(a, b):
    return lax.dot_general(a, b, (((0,), (0,)), ((), ())), preferred_element_type=F32)


def block_at(index, size):
    return pl.ds(pl.multiple_of(index * size, size), size)


def start_all(copies):
    for copy in copies:
        copy.start()
    return copies


def wait_all(copies):
    for copy in copies:
        copy.wait()


def in_vmem(value):
    return pltpu.with_memory_space_constraint(value, pltpu.VMEM)


def in_hbm(value):
    return pltpu.with_memory_space_constraint(value, pltpu.HBM)


def aggregate_rows(a_ref, acat_ref, agg_ref, x_ref, cols, live):
    slots, size = a_ref.shape[1:3]
    for r in range(R):
        acat = jnp.concatenate(
            [jnp.where(k < live(r), a_ref[r, k], jnp.zeros((), BF16)) for k in range(slots)], axis=1
        )
        acat_ref[r] = acat
        for c in range(x_ref.shape[0]):
            picked = jnp.concatenate(
                [x_ref[c, block_at(cols(r, k), size), :] for k in range(slots)], axis=0
            )
            agg_ref[c, r * size : (r + 1) * size, :] = mm(acat, picked).astype(BF16)


def dense_forward(x, agg, cot, ws, wn, wo):
    pre = mm(x, ws) + mm(agg, wn)
    sigma = jax.nn.sigmoid(pre)
    act = (pre * sigma).astype(BF16)
    d_pre = (mm_bt(cot, wo) * sigma * (1.0 + pre * (1.0 - sigma))).astype(BF16)
    return act, d_pre


def add_grads(g_ref, x, agg, act, cot, d_pre, fresh):
    hidden = d_pre.shape[1]
    for p, part in enumerate((mm_at(x, d_pre), mm_at(agg, d_pre), mm_at(act, cot))):
        sl = slice(p * hidden, (p + 1) * hidden)
        if fresh:
            g_ref[sl, :] = part
        else:
            g_ref[sl, :] += part


def send_rows(acc_ref, acat_ref, da_ref, cols, slots):
    clones, _, hidden = acc_ref.shape
    size = acat_ref.shape[1]
    for r in range(R):
        msg = mm_at(acat_ref[r], da_ref[r * size : (r + 1) * size, :])
        for k in range(slots):
            at = block_at(cols(r, k), size)
            for c in range(clones):
                acc_ref[c, at, :] += msg[k * size : (k + 1) * size, c * hidden : (c + 1) * hidden]


def whole_chunk(a_ref, cot_ref, xe, acc, g, upd_ref, acat_s, agg_s, da_s, ws, wn, wo, base, cols, live, fresh, late=()):
    clones, width, hidden = cot_ref.shape
    slots, size = a_ref.shape[1:3]
    rows = pl.ds(pl.multiple_of((base + R) * size, width), width)
    aggregate_rows(a_ref, acat_s, agg_s, xe, cols, live)
    wait_all(late)
    for c in range(clones):
        x, agg, cot = xe[c, rows, :], agg_s[c], cot_ref[c]
        act, d_pre = dense_forward(x, agg, cot, ws[...], wn[...], wo[...])
        upd_ref[c] = (x.astype(F32) + mm(act, wo[...])).astype(BF16)
        add_grads(g, x, agg, act, cot, d_pre, fresh and c == 0)
        da_s[:, c * hidden : (c + 1) * hidden] = mm_bt(d_pre, wn[...]).astype(BF16)
        acc[c, rows, :] += cot.astype(F32) + mm_bt(d_pre, ws[...])
    send_rows(acc, acat_s, da_s, cols, slots)


def mid_kernel(
    idx, cols_ref, cnt_ref, x_hbm, a_hbm, cot_hbm, ws_hbm, wn_hbm, wo_hbm,
    upd_hbm, xe, acc, g, a_near, a_far, cot_near, cot_far, ws, wn, wo,
    a_s, cot_s, upd_s, acat_s, agg_s, da_s, sems,
):
    clones, rows, hidden = x_hbm.shape
    per, slots, size, _ = a_hbm.shape
    width = R * size
    chunks = per // R - 2
    odd = lax.rem(idx[0], 2) == 1
    first = idx[0] * per - R
    near = jnp.where(odd, 0, per - R)
    far = jnp.where(odd, per - R, 0)
    count = iter(range(100))

    def load(source, target):
        copy = pltpu.make_async_copy(source, target, sems.at[next(count)])
        copy.start()
        return copy

    def rows_of(ref, row):
        return ref.at[:, pl.ds(pl.multiple_of(row * size, width), width), :]

    a_in, cot_in, x_in = [], [], []
    x_in.append([load(x_hbm.at[:, : 3 * width, :], xe.at[:, width : 4 * width, :])])
    for i in range(chunks):
        a_in.append(load(a_hbm.at[R + R * i : 2 * R + R * i], a_s.at[i]))
        cot_in.append(load(rows_of(cot_hbm, R + R * i), cot_s.at[i]))
        if i > 0:
            lo, hi = (i + 2) * width, (i + 3) * width
            x_in.append([load(x_hbm.at[:, lo:hi, :], xe.at[:, lo + width : hi + width, :])])
        if i == 0:
            weights = [load(*pair) for pair in ((ws_hbm, ws), (wn_hbm, wn), (wo_hbm, wo))]
    late = [
        load(a_hbm.at[pl.ds(near, R)], a_near),
        load(rows_of(cot_hbm, near), cot_near),
        load(a_hbm.at[pl.ds(far, R)], a_far),
        load(rows_of(cot_hbm, far), cot_far),
    ]
    acc[...] = jnp.zeros_like(acc)
    for i in range(chunks):
        base = R + R * i
        wait_all(x_in[i] + [a_in[i]])
        whole_chunk(
            a_s.at[i], cot_s.at[i], xe, acc, g, upd_s.at[i], acat_s, agg_s, da_s, ws, wn, wo, base,
            lambda r, k: cols_ref[k, base + r] - first, lambda r: cnt_ref[base + r], i == 0,
            [cot_in[i]] + (weights if i == 0 else []),
        )
        late.append(load(upd_s.at[i], rows_of(upd_hbm, base)))
    wait_all(late)


def near_kernel(
    idx, cols_ref, cnt_ref, halo, a_ref, cot_ref, ws, wn, wo, upd_in, xe_in, acc_in, g_in,
    upd_hbm, xe, acc, g, msg_ref,
    upd_s, acat_s, agg_s, da_s, sem,
):
    clones, width, hidden = halo.shape
    size = a_ref.shape[2]
    per = xe.shape[1] // size - 2 * R
    odd = lax.rem(idx[0], 2) == 1
    first = idx[0] * per - R
    base = jnp.where(odd, 0, per - R)
    outer = pl.ds(pl.multiple_of(jnp.where(odd, 0, R + per) * size, width), width)
    xe[:, outer, :] = halo[...]
    whole_chunk(
        a_ref, cot_ref, xe, acc, g, upd_s, acat_s, agg_s, da_s, ws, wn, wo, base,
        lambda r, k: cols_ref[k, base + r] - first, lambda r: cnt_ref[base + r], False,
    )
    store = pltpu.make_async_copy(
        upd_s, upd_hbm.at[:, pl.ds(pl.multiple_of(base * size, width), width), :], sem
    )
    store.start()
    msg_ref[...] = acc[:, outer, :].astype(BF16)
    store.wait()


def far_kernel(
    idx, cols_ref, cnt_ref, halo, a_ref, cot_ref, ws, wn, wo, xe_in, g_in,
    xe, keep_ref, send_ref, act_ref, dpre_ref, acat_ref,
    agg_s, g_s,
):
    clones, width, hidden = halo.shape
    size = a_ref.shape[2]
    per = xe.shape[1] // size - 2 * R
    odd = lax.rem(idx[0], 2)
    first = idx[0] * per - R
    base = jnp.where(odd == 1, per - R, 0)
    outer = pl.ds(pl.multiple_of(jnp.where(odd == 1, R + per, 0) * size, width), width)
    rows = pl.ds(pl.multiple_of((base + R) * size, width), width)
    xe[:, outer, :] = halo[...]
    aggregate_rows(
        a_ref, acat_ref, agg_s, xe,
        lambda r, k: cols_ref[k, base + r] - first, lambda r: cnt_ref[base + r],
    )
    g_s[...] = g_in[...]
    for c in range(clones):
        x, agg, cot = xe[c, rows, :], agg_s[c], cot_ref[c]
        act, d_pre = dense_forward(x, agg, cot, ws[...], wn[...], wo[...])
        act_ref[c] = act
        dpre_ref[c] = d_pre
        add_grads(g_s, x, agg, act, cot, d_pre, False)
    half = g_s.shape[0] // 2
    keep_ref[...] = g_s[pl.ds(pl.multiple_of(odd * half, half), half), :]
    send_ref[...] = g_s[pl.ds(pl.multiple_of((1 - odd) * half, half), half), :]


def message_kernel(idx, cols_ref, dpre, acat, wn, acc_in, acc, msg_ref, da_s):
    clones, width, hidden = dpre.shape
    size = acat.shape[1]
    per = acc.shape[1] // size - 2 * R
    odd = lax.rem(idx[0], 2) == 1
    first = idx[0] * per - R
    base = jnp.where(odd, per - R, 0)
    outer = pl.ds(pl.multiple_of(jnp.where(odd, R + per, 0) * size, width), width)
    for c in range(clones):
        da_s[:, c * hidden : (c + 1) * hidden] = mm_bt(dpre[c], wn[...]).astype(BF16)
    send_rows(acc, acat, da_s, lambda r, k: cols_ref[k, base + r] - first, acat.shape[2] // size)
    msg_ref[...] = acc[:, outer, :].astype(BF16)


def own_kernel(
    idx, nrecv, act, dpre, cot_ref, xe, acc, ws, wo, upd_in,
    upd_hbm, grad_hbm, edge_ref,
    upd_s, grad_s, sems,
):
    clones, width, hidden = act.shape
    rows = upd_hbm.shape[1]
    odd = lax.rem(idx[0], 2) == 1
    far = pl.multiple_of(jnp.where(odd, rows - width, 0), width)
    near = pl.multiple_of(jnp.where(odd, 0, rows - width), width)
    copies = []

    def store(source, target):
        copies.append(pltpu.make_async_copy(source, target, sems.at[len(copies)]))
        copies[-1].start()

    inner = rows - 2 * width
    grad_s[:, :inner, :] = acc[:, 2 * width : 2 * width + inner, :].astype(BF16)
    store(grad_s.at[:, pl.ds(0, inner), :], grad_hbm.at[:, pl.ds(width, inner), :])
    grad_s[:, inner:, :] = (
        acc[:, pl.ds(near + width, width), :] + nrecv[...].astype(F32)
    ).astype(BF16)
    store(grad_s.at[:, pl.ds(inner, width), :], grad_hbm.at[:, pl.ds(near, width), :])
    for c in range(clones):
        x = xe[c, pl.ds(far + width, width), :]
        upd_s[c] = (x.astype(F32) + mm(act[c], wo[...])).astype(BF16)
    store(upd_s, upd_hbm.at[:, pl.ds(far, width), :])
    for c in range(clones):
        edge_ref[c] = (
            acc[c, pl.ds(far + width, width), :] + cot_ref[c].astype(F32) + mm_bt(dpre[c], ws[...])
        )
    wait_all(copies)


def edge_kernel(idx, edge_ref, frecv_ref, grad_in, grad_hbm, out_s, sem):
    rows, width = grad_hbm.shape[1], edge_ref.shape[1]
    start = pl.multiple_of(jnp.where(lax.rem(idx[0], 2) == 1, rows - width, 0), width)
    out_s[...] = (edge_ref[...] + frecv_ref[...].astype(F32)).astype(BF16)
    out = pltpu.make_async_copy(out_s, grad_hbm.at[:, pl.ds(start, width), :], sem)
    out.start()
    out.wait()


def swap(value, bit):
    count = lax.axis_size("dom")
    return lax.ppermute(value, "dom", [(i, i ^ bit) for i in range(count)])


def half_rows(ref, bit):
    half = ref.shape[0] // 2
    return pl.ds(pl.multiple_of(bit * half, half), half)


def bit_of(idx, shift):
    return lax.rem(lax.shift_right_logical(idx[0], shift), 2)


def scatter_kernel(shift, idx, mine, other, keep_ref, send_ref):
    bit = bit_of(idx, shift)
    stay, leave = half_rows(mine, bit), half_rows(mine, 1 - bit)
    send_ref[...] = (mine[leave, :] + other[leave, :].astype(F32)).astype(BF16)
    keep_ref[...] = mine[stay, :] + other[stay, :].astype(F32)


def add_kernel(mine, other, out_ref):
    out_ref[...] = (mine[...].astype(F32) + other[...].astype(F32)).astype(BF16)


def join_kernel(shift, idx, mine, other, out_ref):
    bit = bit_of(idx, shift)
    out_ref[half_rows(out_ref, bit), :] = mine[...]
    out_ref[half_rows(out_ref, 1 - bit), :] = other[...]


def final_kernel(factor, idx, mine, other, gs_ref, gn_ref, go_ref, all_s):
    join_kernel(0, idx, mine, other, all_s)
    hidden = gs_ref.shape[0]
    for p, ref in enumerate((gs_ref, gn_ref, go_ref)):
        ref[...] = all_s[p * hidden : (p + 1) * hidden, :].astype(F32) * factor


def reduce_all(call, keep, send, idx, factor, hooks):
    count = lax.axis_size("dom")
    hidden = keep.shape[1]
    stage = iter(range(100))
    sds = jax.ShapeDtypeStruct

    def vm(rows, kind):
        return pltpu.VMEM((rows, hidden), kind)

    def exchange(value, shift):
        moved = swap(value, 1 << shift)
        for hook in hooks.get(next(stage), ()):
            moved = hook(value, moved)
        return in_vmem(moved)

    mine, other = keep, exchange(send, 0)
    shifts = list(range(1, count.bit_length() - 1))
    scatter = shifts[1:2]
    for shift in scatter:
        rows = mine.shape[0] // 2
        mine, out = call(
            functools.partial(scatter_kernel, shift), "scatter", (idx, mine, other),
            [SM, VM, VM], (vm(rows, F32), vm(rows, BF16)), (VM, VM), [],
        )
        other = exchange(out, shift)
    for shift in [None] + [s for s in reversed(shifts) if s not in scatter]:
        if shift is not None:
            other = exchange(mine, shift)
        mine = call(add_kernel, "add", (mine, other), [VM, VM], vm(mine.shape[0], BF16), VM, [])
    for shift in reversed(scatter):
        other = exchange(mine, shift)
        mine = call(
            functools.partial(join_kernel, shift), "join", (idx, mine, other),
            [SM, VM, VM], vm(2 * mine.shape[0], BF16), VM, [],
        )
    other = exchange(mine, 0)
    return call(
        functools.partial(final_kernel, factor), "final", (idx, mine, other),
        [SM, VM, VM], (sds((hidden, hidden), F32),) * 3, (VM,) * 3, [vm(3 * hidden, BF16)],
    )


def body(features, cotangent, adjacency, tile_cols, tile_counts, w_self, w_neigh, w_out):
    clones, rows, hidden = features.shape
    per, slots, size, _ = adjacency.shape
    width = R * size
    chunks = per // R - 2
    count = lax.axis_size("dom")
    index = lax.axis_index("dom")
    odd = (index & 1) == 1
    idx = index.reshape(1).astype(jnp.int32)
    cols = tile_cols.T
    near_pairs = [(i, i ^ 1) for i in range(count)]
    far_pairs = [(i, ((i + 1) ^ 1) - 1) for i in range(1, count - 1)]
    far_out = lax.dynamic_slice_in_dim(features, jnp.where(odd, rows - width, 0), width, axis=1)
    far_halo = lax.ppermute(far_out, "dom", far_pairs)
    near_out = lax.dynamic_slice_in_dim(features, jnp.where(odd, 0, rows - width), width, axis=1)
    near_halo = lax.ppermute(near_out, "dom", near_pairs)

    sds = jax.ShapeDtypeStruct
    full = sds((clones, rows, hidden), BF16)
    strip = pltpu.VMEM((clones, width, hidden), BF16)
    xe_t = pltpu.VMEM((clones, rows + 2 * width, hidden), BF16)
    acc_t = pltpu.VMEM((clones, rows + 2 * width, hidden), F32)
    g_t = pltpu.VMEM((3 * hidden, hidden), F32)
    half_t = pltpu.VMEM((3 * hidden // 2, hidden), F32)
    a_t = pltpu.VMEM((R, slots, size, size), BF16)
    acat_t = pltpu.VMEM((R, size, slots * size), BF16)
    da_t = pltpu.VMEM((width, clones * hidden), BF16)

    def call(kernel, name, ins, in_specs, outs, out_specs, scratch, aliases=None):
        return pl.pallas_call(
            kernel,
            out_shape=outs,
            in_specs=in_specs,
            out_specs=out_specs,
            scratch_shapes=scratch,
            input_output_aliases=aliases or {},
            compiler_params=pltpu.CompilerParams(vmem_limit_bytes=LIMIT),
            cost_estimate=pl.CostEstimate(flops=COSTS.get(name, 1), transcendentals=0, bytes_accessed=0),
            name=name,
        )(*ins)

    w_t = pltpu.VMEM((hidden, hidden), BF16)
    big = tuple(in_hbm(v) for v in (features, adjacency, cotangent, w_self, w_neigh, w_out))
    upd, xe, acc, g, a_near, a_far, cot_near, cot_far, ws, wn, wo = call(
        mid_kernel, "mid_rows",
        (idx, cols, tile_counts) + big,
        [SM] * 3 + [ANY] * 6,
        (full, xe_t, acc_t, g_t, a_t, a_t, strip, strip, w_t, w_t, w_t),
        (ANY,) + (VM,) * 10,
        [
            pltpu.VMEM((chunks, R, slots, size, size), BF16),
            pltpu.VMEM((chunks, clones, width, hidden), BF16),
            pltpu.VMEM((chunks, clones, width, hidden), BF16),
            acat_t, strip, da_t,
            pltpu.SemaphoreType.DMA((4 * chunks + 7,)),
        ],
    )
    upd, xe, acc, g, near_msg = call(
        near_kernel, "near_rows",
        (idx, cols, tile_counts, in_vmem(near_halo), a_near, cot_near, ws, wn, wo, upd, xe, acc, g),
        [SM] * 3 + [VM] * 6 + [ANY] + [VM] * 3,
        (full, xe_t, acc_t, g_t, strip),
        (ANY,) + (VM,) * 4,
        [strip, acat_t, strip, da_t, pltpu.SemaphoreType.DMA],
        {9: 0, 10: 1, 11: 2, 12: 3},
    )
    near_recv = lax.ppermute(near_msg, "dom", near_pairs)
    xe, keep, send, act, d_pre, acat = call(
        far_kernel, "far_rows",
        (idx, cols, tile_counts, in_vmem(far_halo), a_far, cot_far, ws, wn, wo, xe, g),
        [SM] * 3 + [VM] * 8,
        (xe_t, half_t, half_t, strip, strip, acat_t),
        (VM,) * 6,
        [strip, g_t],
        {9: 0},
    )
    kept = {}

    def held(value, before):
        value, before = lax.optimization_barrier((value, before))
        return value, before

    def message(after, before):
        gate, _ = lax.optimization_barrier((idx, after))
        kept["acc"], msg = call(
            message_kernel, "messages",
            (gate, cols, d_pre, acat, wn, acc),
            [SM] * 2 + [VM] * 4,
            (acc_t, strip),
            (VM, VM),
            [da_t],
            {5: 0},
        )
        kept["msg"], before = held(msg, before)
        return before

    def far_send(after, before):
        msg, _ = lax.optimization_barrier((kept["msg"], after))
        kept["recv"] = lax.ppermute(msg, "dom", far_pairs)
        return before

    def own(after, before):
        gate, _ = lax.optimization_barrier((idx, after))
        kept["upd"], grad, kept["edge"] = call(
            own_kernel, "own_rows",
            (gate, in_vmem(near_recv), act, d_pre, cot_far, xe, kept["acc"], ws, wo, upd),
            [SM] + [VM] * 8 + [ANY],
            (full, full, pltpu.VMEM((clones, width, hidden), F32)),
            (ANY, ANY, VM),
            [strip, pltpu.VMEM((clones, rows - width, hidden), BF16), pltpu.SemaphoreType.DMA((3,))],
            {9: 0},
        )
        kept["grad"], before = held(grad, before)
        return before

    def edge(after, before):
        gate, _ = lax.optimization_barrier((idx, after))
        grad = call(
            edge_kernel, "edge_rows",
            (gate, kept["edge"], in_vmem(kept["recv"]), kept["grad"]),
            [SM, VM, VM, ANY],
            full,
            ANY,
            [strip, pltpu.SemaphoreType.DMA],
            {3: 0},
        )
        kept["grad"], before = held(grad, before)
        return before

    factor = 1.0 / math.sqrt(2.0 * rows * count)
    hooks = {0: (message,), 1: (far_send,)}
    for at, hook in ((OWN_AT, own), (EDGE_AT, edge)):
        hooks[at] = hooks.get(at, ()) + (hook,)
    sums = reduce_all(call, keep, send, idx, factor, hooks)
    return (
        kept["upd"],
        kept["grad"],
        *sums,
    )


def solution(mesh):
    return jax.shard_map(
        body,
        mesh=mesh,
        in_specs=(
            P("groups", "dom", None),
            P("groups", "dom", None),
            P("dom", None, None, None),
            P("dom", None),
            P("dom"),
            P(),
            P(),
            P(),
        ),
        out_specs=(
            P("groups", "dom", None),
            P("groups", "dom", None),
            P("groups", None),
            P("groups", None),
            P("groups", None),
        ),
        check_vma=False,
    )
```

time: 224 us -> 56.9 us (0.25)
  waiting for transfers between devices: 82.9 us -> 20.8 us
  matrix products: 57.2 us -> 0 us
  local copies, waits for them, and re-layouts: 42.8 us -> 1.29 us
  Pallas kernels: 0 us -> 20.8 us
  between operations: 14.3 us -> 0.82 us
  other arithmetic: 11.4 us -> 0 us
    psum x1 -> x0, waiting for transfers between devices: 82.9 us -> none  [body(): lax.psum((jnp.dot(activated.T, flat_cot, preferred_element_type=jnp.float...]
    dot_general x12 -> x0, matrix products: 57.2 us -> none  [the longest x1 22.7 us: fold_rows(): jnp.einsum('ms,cmjf->csjf', one_hot, contrib_rows, precision=lax.Precisio...]
    pallas_call x0 -> x12, Pallas kernels: none -> 20.8 us  [call(): pl.pallas_call(kernel, out_shape=outs, in_specs=in_specs, out_specs=out_s...]
    ppermute x4 -> x10, waiting for transfers between devices: 0.01 us -> 20.8 us  [the longest x6 20.8 us: swap(): return lax.ppermute(value, 'dom', [(i, i ^ bit) for i in range(count)])]
    transpose x1 -> x0, local copies, waits for them, and re-layouts: 18 us -> none  [body(): jnp.einsum('rkij,crif->crkjf', live_tiles, d_blocks, preferred_element_ty...]
    slice x3 -> x0, local copies, waits for them, and re-layouts: 7.61 us -> none  [the longest x1 2.91 us: body(): from_above = shifted(summed[:, :R].astype(jnp.bfloat16), 'dom', -1)]
    unnamed x35 -> x4, local copies, waits for them, and re-layouts: 6.27 us -> 0.01 us
    scatter-add x2 -> x0, other arithmetic: 5.91 us -> none  [the longest x1 2.96 us: body(): center = center.at[:, :R].add(from_below.astype(jnp.float32))]
  transfers between devices with their start and end apart: 5 -> 10, of which waited for: 1 -> 5; matrix products, arithmetic and copies ran while one was open for 10% -> 0% of each run, Pallas kernels for 0% -> 31%
where the time goes in v2:
time: 56.9 us; the launch traced here: 56.8 us
  Pallas kernels  20.8 us (37%)
  waiting for transfers between devices  20.8 us (37%)
  starting transfers between devices  13.1 us (23%)
  local copies, waits for them, and re-layouts  1.29 us (2%)
  between operations  0.82 us (1%)
    pallas_call x12, Pallas kernels, call(): pl.pallas_call(kernel, out_shape=outs, in_specs=in_specs, out_specs=out_s...  20.8 us
    ppermute x6, waiting for transfers between devices, swap(): return lax.ppermute(value, 'dom', [(i, i ^ bit) for i in range(count)])  20.8 us
    ppermute x6, starting transfers between devices, swap(): return lax.ppermute(value, 'dom', [(i, i ^ bit) for i in range(count)])  11.1 us
    dynamic_slice x1, local copies, waits for them, and re-layouts, body(): lax.dynamic_slice_in_dim(features, jnp.where(odd, 0, rows - width), width...  1.28 us
  transfers between devices with their start and end apart: 10, of which 5 were waited for; matrix products, arithmetic and copies ran while one was open for 0% of the time, Pallas kernels for 31%

profile of v2, /device:TPU:0, one launch (start us, length us, event | category | flops | bytes accessed | tf_op | source)
XLA Modules:
  0.0 56.8 jit_solution(11617301549200945630)
XLA Ops:
  0.7 1.3 %constant_dynamic-slice_fusion = (bf16[2,512,256]{2,1,0:T(8,128)(2,1)S(1)}, bf16[2,512,256]{2,1,0:T(8,128)(2,1)S(1)}) fusion(bf16[2,2048,256]{2,1,0:T(8,128)(2,1)} %x_hbm.1, s32[]{:T(128)S(6)} %select_n.10, s32[]{:T(128)S(6)} %select_n.9), kind=kLoop, calls=%fused_computation | loop fusion | bytes 2097160 | tf_op jit(solution)/shard_map/dynamic_slice | solution.py:374
  1.9 0.5 collective-permute-start.1
  2.5 0.7 %collective-permute-start = (bf16[2,512,256]{2,1,0:T(8,128)(2,1)S(1)}, bf16[2,512,256]{2,1,0:T(8,128)(2,1)S(1)}, u32[]{:S(2)}, u32[]{:S(2)}) collective-permute-start(bf16[2,512,256]{2,1,0:T(8,128)(2,1)S(1)} %get-tuple-element.90), channel_id=1, source_target_pairs={{1,2},{2,1},{3,4},{4,3},{5,6},{6,5},{7,8},{8,7},{9,10},{10,9},{11,... | collective-permute-start | bytes 1572872 | tf_op jit(solution)/shard_map/ppermute | solution.py:373
  3.2 8.9 %mid_rows.1 = (bf16[2,2048,256]{2,1,0:T(8,128)(2,1)}, bf16[2,3072,256]{2,1,0:T(8,128)(2,1)S(1)}, f32[2,3072,256]{2,1,0:T(8,128)S(1)}, f32[768,256]{1,0:T(8,128)S...) custom-call(s32[1]{0:T(128)} %bitcast.idx, ...), custom_call_target="tpu_custom_call" | custom-call | flops 1 | tf_op jit(solution)/shard_map/mid_rows/pallas_call | solution.py:389
  12.1 0.0 collective-permute-done.1.halo
  12.1 4.1 %near_rows.1 = (bf16[2,2048,256]{2,1,0:T(8,128)(2,1)}, bf16[2,3072,256]{2,1,0:T(8,128)(2,1)S(1)}, f32[2,3072,256]{2,1,0:T(8,128)S(1)}, f32[768,256]{1,0:T(8,128)S(1)}, bf16[2,512,256]{2,1,0:T(8,128)(2,1)S(1)}) custom-call(s32[1]{0:T(128)} %bitcast.idx, ...), custom_call_target="tpu_custom_call", output_to_operand_aliasing={{0}: (9, {}), {1}: (10, {}), {2}: (11, {}), {3}: (12, {})} | custom-call | flops 1 | tf_op jit(solution)/shard_map/near_rows/pallas_call | solution.py:389
  16.2 2.4 %far_rows.1 = (bf16[2,3072,256]{2,1,0:T(8,128)(2,1)S(1)}, f32[384,256]{1,0:T(8,128)S(1)}, f32[384,256]{1,0:T(8,128)S(1)}, bf16[2,512,256]{2,1,0:T(8,128)(2,1)S(1...) custom-call(s32[1]{0:T(128)} %bitcast.idx, ...), custom_call_target="tpu_custom_call", output_to_operand_aliasing={{0}: (9, {})} | custom-call | flops 1 | tf_op jit(solution)/shard_map/far_rows/pallas_call | solution.py:389
  18.6 3.9 %collective-permute-start.2 = (f32[384,256]{1,0:T(8,128)S(1)}, f32[384,256]{1,0:T(8,128)S(1)}, u32[]{:S(2)}, u32[]{:S(2)}) collective-permute-start(f32[384,256]{1,0:T(8,128)S(1)} %get-tuple-element.61), channel_id=1, source_target_pairs={{0,1},{1,0},{2,3},{3,2},{4,5},{5,4},{6,7},{7,6},{8,9},{9,8},{10,11... | collective-permute-start | bytes 1179656 | tf_op jit(solution)/shard_map/ppermute | solution.py:282
  22.6 0.1 collective-permute-start.4
  22.7 1.5 %messages.1 = (f32[2,3072,256]{2,1,0:T(8,128)S(1)}, bf16[2,512,256]{2,1,0:T(8,128)(2,1)S(1)}) custom-call(s32[1]{0:T(128)} %bitcast.idx, s32[4,16]{1,0:T(4,128)S(1)} %bitcast.5, bf16[2,512,256]{2,1,0:T(8,128)(2,1)S(1)} %get-tuple-element.63.dpre, bf16[4,128,512]{2,1,0:T(8,128)(2,1)S(1)} %get-tuple-element.64.acat, ...), custom_call_target="tpu_custom_call", output_to_operand_aliasing={{0}: (5, {})} | custom-call | flops 1 | tf_op jit(solution)/shard_map/messages/pallas_call | solution.py:389
  24.2 0.7 %collective-permute-start.6 = (bf16[2,512,256]{2,1,0:T(8,128)(2,1)S(1)}, bf16[2,512,256]{2,1,0:T(8,128)(2,1)S(1)}, u32[]{:S(2)}, u32[]{:S(2)}) collective-permute-start(bf16[2,512,256]{2,1,0:T(8,128)(2,1)S(1)} %get-tuple-element.82), channel_id=1, source_target_pairs={{1,2},{2,1},{3,4},{4,3},{5,6},{6,5},{7,8},{8,7},{9,10},{10,9},{11,... | collective-permute-start | bytes 1572872 | tf_op jit(solution)/shard_map/ppermute | solution.py:458
  24.9 4.3 %collective-permute-start.3 = (bf16[192,256]{1,0:T(8,128)(2,1)S(1)}, bf16[192,256]{1,0:T(8,128)(2,1)S(1)}, u32[]{:S(2)}, u32[]{:S(2)}) collective-permute-start(bf16[192,256]{1,0:T(8,128)(2,1)S(1)} %get-tuple-element.69), channel_id=1, source_target_pairs={{0,4},{1,5},{2,6},{3,7},{4,0},{5,1},{6,2},{7,3},{8,12},{9,13},{10,... | collective-permute-start | bytes 294920 | tf_op jit(solution)/shard_map/ppermute | solution.py:282
  29.2 10.0 %collective-permute-done.3.other = bf16[192,256]{1,0:T(8,128)(2,1)S(1)} collective-permute-done((bf16[192,256]{1,0:T(8,128)(2,1)S(1)}, bf16[192,256]{1,0:T(8,128)(2,1)S(1)}, u32[]{:S(2)}, u32[]{:S(2)}) %collective-permute-start.3) | collective-permute-done | bytes 98336 | tf_op jit(solution)/shard_map/ppermute | solution.py:282
  39.3 2.7 %collective-permute-start.5 = (bf16[192,256]{1,0:T(8,128)(2,1)S(1)}, bf16[192,256]{1,0:T(8,128)(2,1)S(1)}, u32[]{:S(2)}, u32[]{:S(2)}) collective-permute-start(bf16[192,256]{1,0:T(8,128)(2,1)S(1)} %add.5.mine), channel_id=1, source_target_pairs={{0,8},{1,9},{2,10},{3,11},{4,12},{5,13},{6,14},{7,15},{8,0},{9,1},... | collective-permute-start | bytes 294920 | tf_op jit(solution)/shard_map/ppermute | solution.py:282
  42.0 1.9 %own_rows.1 = (bf16[2,2048,256]{2,1,0:T(8,128)(2,1)}, bf16[2,2048,256]{2,1,0:T(8,128)(2,1)}, f32[2,512,256]{2,1,0:T(8,128)S(1)}) custom-call(s32[1]{0:T(128)} %bitcast.idx, bf16[2,512,256]{2,1,0:T(8,128)(2,1)S(1)} %collective-permute-done.4.nrecv, bf16[2,512,256]{2,1,0:T(8,128)(2,1)S(1)} %get-tuple-element.72.act, ...), custom_call_target="tpu_custom_call", output_to_operand_aliasing={{0}: (9, {})} | custom-call | flops 1 | tf_op jit(solution)/shard_map/own_rows/pallas_call | solution.py:389
  43.9 1.0 %collective-permute-done.5.other = bf16[192,256]{1,0:T(8,128)(2,1)S(1)} collective-permute-done((bf16[192,256]{1,0:T(8,128)(2,1)S(1)}, bf16[192,256]{1,0:T(8,128)(2,1)S(1)}, u32[]{:S(2)}, u32[]{:S(2)}) %collective-permute-start.5) | collective-permute-done | bytes 98336 | tf_op jit(solution)/shard_map/ppermute | solution.py:282
  44.9 0.1 collective-permute-start.7
  45.0 0.9 %edge_rows.1 = bf16[2,2048,256]{2,1,0:T(8,128)(2,1)} custom-call(s32[1]{0:T(128)} %bitcast.idx, f32[2,512,256]{2,1,0:T(8,128)S(1)} %get-tuple-element.80.edge_ref, bf16[2,512,256]{2,1,0:T(8,128)(2,1)S(1)} %collective-permute-done.6.frecv_ref, bf16[2,2048,256]{2,1,0:T(8,128)(2,1)} %get-tuple-element.83.grad_in), custom_call_target="tpu_custom_call", output_to_operand_aliasing={{}: (3, {})} | custom-call | flops 1 | tf_op jit(solution)/shard_map/edge_rows/pallas_call | solution.py:389
  45.9 3.7 %collective-permute-done.7.other = bf16[192,256]{1,0:T(8,128)(2,1)S(1)} collective-permute-done((bf16[192,256]{1,0:T(8,128)(2,1)S(1)}, bf16[192,256]{1,0:T(8,128)(2,1)S(1)}, u32[]{:S(2)}, u32[]{:S(2)}) %collective-permute-start.7) | collective-permute-done | bytes 98336 | tf_op jit(solution)/shard_map/ppermute | solution.py:282
  49.6 0.1 collective-permute-start.8
  49.7 4.6 %collective-permute-done.8.other = bf16[192,256]{1,0:T(8,128)(2,1)S(1)} collective-permute-done((bf16[192,256]{1,0:T(8,128)(2,1)S(1)}, bf16[192,256]{1,0:T(8,128)(2,1)S(1)}, u32[]{:S(2)}, u32[]{:S(2)}) %collective-permute-start.8) | collective-permute-done | bytes 98336 | tf_op jit(solution)/shard_map/ppermute | solution.py:282
  54.3 0.1 collective-permute-start.9
  54.4 1.4 %collective-permute-done.9.other = bf16[384,256]{1,0:T(8,128)(2,1)S(1)} collective-permute-done((bf16[384,256]{1,0:T(8,128)(2,1)S(1)}, bf16[384,256]{1,0:T(8,128)(2,1)S(1)}, u32[]{:S(2)}, u32[]{:S(2)}) %collective-permute-start.9) | collective-permute-done | bytes 196640 | tf_op jit(solution)/shard_map/ppermute | solution.py:282
  55.8 0.9 %final.1 = (f32[256,256]{1,0:T(8,128)}, f32[256,256]{1,0:T(8,128)}, f32[256,256]{1,0:T(8,128)}) custom-call(s32[1]{0:T(128)} %bitcast.idx, bf16[384,256]{1,0:T(8,128)(2,1)S(1)} %join.1.mine, bf16[384,256]{1,0:T(8,128)(2,1)S(1)} %collective-permute-done.9.other), custom_call_target="tpu_custom_call" | custom-call | flops 1 | tf_op jit(solution)/shard_map/final/pallas_call | solution.py:389
  (13 shorter events, 0.2 us)
Async XLA Ops:
  0.6 2.5 %copy-start.1 = (s32[16]{0:T(128)S(1)}, s32[16]{0:T(128)}, u32[]{:S(2)}) copy-start(s32[16]{0:T(128)} %cnt_ref.5) | copy-start | bytes 196
  0.6 2.5 %copy-start = (s32[16,4]{0,1:T(4,128)S(1)}, s32[16,4]{0,1:T(4,128)}, u32[]{:S(2)}) copy-start(s32[16,4]{0,1:T(4,128)} %param.11) | copy-start | bytes 772
  1.9 10.1 %collective-permute-start.1 = (bf16[2,512,256]{2,1,0:T(8,128)(2,1)S(1)}, bf16[2,512,256]{2,1,0:T(8,128)(2,1)S(1)}, u32[]{:S(2)}, u32[]{:S(2)}) collective-permute-start(bf16[2,512,256]{2,1,0:T(8,128)(2,1)S(1)} %get-tuple-element.89), channel_id=1, source_target_pairs={{0,1},{1,0},{2,3},{3,2},{4,5},{5,4},{6,7},{7,6},{8,9},{9,8},{10,11... | collective-permute-start | bytes 1572872 | tf_op jit(solution)/shard_map/ppermute | solution.py:375
  2.5 13.7 %collective-permute-start = (bf16[2,512,256]{2,1,0:T(8,128)(2,1)S(1)}, bf16[2,512,256]{2,1,0:T(8,128)(2,1)S(1)}, u32[]{:S(2)}, u32[]{:S(2)}) collective-permute-start(bf16[2,512,256]{2,1,0:T(8,128)(2,1)S(1)} %get-tuple-element.90), channel_id=1, source_target_pairs={{1,2},{2,1},{3,4},{4,3},{5,6},{6,5},{7,8},{8,7},{9,10},{10,9},{11,... | collective-permute-start | bytes 1572872 | tf_op jit(solution)/shard_map/ppermute | solution.py:373
  18.6 5.5 %collective-permute-start.2 = (f32[384,256]{1,0:T(8,128)S(1)}, f32[384,256]{1,0:T(8,128)S(1)}, u32[]{:S(2)}, u32[]{:S(2)}) collective-permute-start(f32[384,256]{1,0:T(8,128)S(1)} %get-tuple-element.61), channel_id=1, source_target_pairs={{0,1},{1,0},{2,3},{3,2},{4,5},{5,4},{6,7},{7,6},{8,9},{9,8},{10,11... | collective-permute-start | bytes 1179656 | tf_op jit(solution)/shard_map/ppermute | solution.py:282
  22.6 19.4 %collective-permute-start.4 = (bf16[2,512,256]{2,1,0:T(8,128)(2,1)S(1)}, bf16[2,512,256]{2,1,0:T(8,128)(2,1)S(1)}, u32[]{:S(2)}, u32[]{:S(2)}) collective-permute-start(bf16[2,512,256]{2,1,0:T(8,128)(2,1)S(1)} %get-tuple-element.71), channel_id=1, source_target_pairs={{0,1},{1,0},{2,3},{3,2},{4,5},{5,4},{6,7},{7,6},{8,9},{9,8},{10,11... | collective-permute-start | bytes 1572872 | tf_op jit(solution)/shard_map/ppermute | solution.py:426
  24.2 20.8 %collective-permute-start.6 = (bf16[2,512,256]{2,1,0:T(8,128)(2,1)S(1)}, bf16[2,512,256]{2,1,0:T(8,128)(2,1)S(1)}, u32[]{:S(2)}, u32[]{:S(2)}) collective-permute-start(bf16[2,512,256]{2,1,0:T(8,128)(2,1)S(1)} %get-tuple-element.82), channel_id=1, source_target_pairs={{1,2},{2,1},{3,4},{4,3},{5,6},{6,5},{7,8},{8,7},{9,10},{10,9},{11,... | collective-permute-start | bytes 1572872 | tf_op jit(solution)/shard_map/ppermute | solution.py:458
  24.9 14.3 %collective-permute-start.3 = (bf16[192,256]{1,0:T(8,128)(2,1)S(1)}, bf16[192,256]{1,0:T(8,128)(2,1)S(1)}, u32[]{:S(2)}, u32[]{:S(2)}) collective-permute-start(bf16[192,256]{1,0:T(8,128)(2,1)S(1)} %get-tuple-element.69), channel_id=1, source_target_pairs={{0,4},{1,5},{2,6},{3,7},{4,0},{5,1},{6,2},{7,3},{8,12},{9,13},{10,... | collective-permute-start | bytes 294920 | tf_op jit(solution)/shard_map/ppermute | solution.py:282
  39.3 5.6 %collective-permute-start.5 = (bf16[192,256]{1,0:T(8,128)(2,1)S(1)}, bf16[192,256]{1,0:T(8,128)(2,1)S(1)}, u32[]{:S(2)}, u32[]{:S(2)}) collective-permute-start(bf16[192,256]{1,0:T(8,128)(2,1)S(1)} %add.5.mine), channel_id=1, source_target_pairs={{0,8},{1,9},{2,10},{3,11},{4,12},{5,13},{6,14},{7,15},{8,0},{9,1},... | collective-permute-start | bytes 294920 | tf_op jit(solution)/shard_map/ppermute | solution.py:282
  44.9 4.7 %collective-permute-start.7 = (bf16[192,256]{1,0:T(8,128)(2,1)S(1)}, bf16[192,256]{1,0:T(8,128)(2,1)S(1)}, u32[]{:S(2)}, u32[]{:S(2)}) collective-permute-start(bf16[192,256]{1,0:T(8,128)(2,1)S(1)} %add.6.mine), channel_id=1, source_target_pairs={{0,2},{1,3},{2,0},{3,1},{4,6},{5,7},{6,4},{7,5},{8,10},{9,11},{10,... | collective-permute-start | bytes 294920 | tf_op jit(solution)/shard_map/ppermute | solution.py:282
  49.6 4.7 %collective-permute-start.8 = (bf16[192,256]{1,0:T(8,128)(2,1)S(1)}, bf16[192,256]{1,0:T(8,128)(2,1)S(1)}, u32[]{:S(2)}, u32[]{:S(2)}) collective-permute-start(bf16[192,256]{1,0:T(8,128)(2,1)S(1)} %add.7.mine), channel_id=1, source_target_pairs={{0,4},{1,5},{2,6},{3,7},{4,0},{5,1},{6,2},{7,3},{8,12},{9,13},{10,... | collective-permute-start | bytes 294920 | tf_op jit(solution)/shard_map/ppermute | solution.py:282
  54.3 1.5 %collective-permute-start.9 = (bf16[384,256]{1,0:T(8,128)(2,1)S(1)}, bf16[384,256]{1,0:T(8,128)(2,1)S(1)}, u32[]{:S(2)}, u32[]{:S(2)}) collective-permute-start(bf16[384,256]{1,0:T(8,128)(2,1)S(1)} %join.1.mine), channel_id=1, source_target_pairs={{0,1},{1,0},{2,3},{3,2},{4,5},{5,4},{6,7},{7,6},{8,9},{9,8},{10,11... | collective-permute-start | bytes 589832 | tf_op jit(solution)/shard_map/ppermute | solution.py:282

commit v3 on v2

--- a/solution.py
+++ b/solution.py
@@ -14,7 +14,7 @@
 ANY = pl.BlockSpec(memory_space=pltpu.HBM)
 VM = pl.BlockSpec(memory_space=pltpu.VMEM)
 SM = pl.BlockSpec(memory_space=pltpu.SMEM)
-OWN_AT, EDGE_AT = 2, 3
+OWN_AT, EDGE_AT = 2, 4
 COSTS = dict(mid_rows=1, near_rows=1, far_rows=1, messages=1, own_rows=1, edge_rows=1)
 LIMIT = 12 * 1024 * 1024
 
@@ -268,10 +268,11 @@
     wait_all(copies)
 
 
-def edge_kernel(idx, edge_ref, frecv_ref, grad_in, grad_hbm, out_s, sem):
+def edge_kernel(idx, edge_ref, straight_ref, across_ref, grad_in, grad_hbm, out_s, sem):
     rows, width = grad_hbm.shape[1], edge_ref.shape[1]
     start = pl.multiple_of(jnp.where(lax.rem(idx[0], 2) == 1, rows - width, 0), width)
-    out_s[...] = (edge_ref[...] + frecv_ref[...].astype(F32)).astype(BF16)
+    received = straight_ref[...].astype(F32) + across_ref[...].astype(F32)
+    out_s[...] = (edge_ref[...] + received).astype(BF16)
     out = pltpu.make_async_copy(out_s, grad_hbm.at[:, pl.ds(start, width), :], sem)
     out.start()
     out.wait()
@@ -453,10 +454,13 @@
         kept["msg"], before = held(msg, before)
         return before
 
-    def far_send(after, before):
-        msg, _ = lax.optimization_barrier((kept["msg"], after))
-        kept["recv"] = lax.ppermute(msg, "dom", far_pairs)
-        return before
+    def send_far(name, sides):
+        def hook(after, before):
+            msg, _ = lax.optimization_barrier((kept["msg"], after))
+            kept[name] = lax.ppermute(msg, "dom", [p for p in far_pairs if p[0] % 4 in sides])
+            return before
+
+        return hook
 
     def own(after, before):
         gate, _ = lax.optimization_barrier((idx, after))
@@ -476,18 +480,18 @@
         gate, _ = lax.optimization_barrier((idx, after))
         grad = call(
             edge_kernel, "edge_rows",
-            (gate, kept["edge"], in_vmem(kept["recv"]), kept["grad"]),
-            [SM, VM, VM, ANY],
+            (gate, kept["edge"], in_vmem(kept["straight"]), in_vmem(kept["across"]), kept["grad"]),
+            [SM, VM, VM, VM, ANY],
             full,
             ANY,
             [strip, pltpu.SemaphoreType.DMA],
-            {3: 0},
+            {4: 0},
         )
         kept["grad"], before = held(grad, before)
         return before
 
     factor = 1.0 / math.sqrt(2.0 * rows * count)
-    hooks = {0: (message,), 1: (far_send,)}
+    hooks = {0: (message, send_far("across", (0, 3)),), 2: (send_far("straight", (1, 2)),)}
     for at, hook in ((OWN_AT, own), (EDGE_AT, edge)):
         hooks[at] = hooks.get(at, ()) + (hook,)
     sums = reduce_all(call, keep, send, idx, factor, hooks)

time: 56.9 us -> 54.1 us (0.951)
  starting transfers between devices: 13.1 us -> 11.4 us
  waiting for transfers between devices: 20.8 us -> 19.5 us
    ppermute x6, starting transfers between devices: 11.1 us -> 8.75 us  [swap(): return lax.ppermute(value, 'dom', [(i, i ^ bit) for i in range(count)])]
    ppermute x6, waiting for transfers between devices: 20.8 us -> 19.5 us  [swap(): return lax.ppermute(value, 'dom', [(i, i ^ bit) for i in range(count)])]
    ppermute x1 -> x2, starting transfers between devices: 0.69 us -> 1.38 us  [hook(): lax.ppermute(msg, 'dom', [p for p in far_pairs if p[0] % 4 in sides])]
  transfers between devices with their start and end apart: 10 -> 11, of which waited for: 5 -> 5; matrix products, arithmetic and copies ran while one was open for 0% -> 0% of each run, Pallas kernels for 31% -> 32%
where the time goes in v3:
time: 54.1 us; the launch traced here: 53.9 us
  Pallas kernels  20.9 us (39%)
  waiting for transfers between devices  19.5 us (36%)
  starting transfers between devices  11.4 us (21%)
  local copies, waits for them, and re-layouts  1.29 us (2%)
  between operations  0.83 us (2%)
    pallas_call x12, Pallas kernels, call(): pl.pallas_call(kernel, out_shape=outs, in_specs=in_specs, out_specs=out_s...  20.9 us
    ppermute x6, waiting for transfers between devices, swap(): return lax.ppermute(value, 'dom', [(i, i ^ bit) for i in range(count)])  19.5 us
    ppermute x6, starting transfers between devices, swap(): return lax.ppermute(value, 'dom', [(i, i ^ bit) for i in range(count)])  8.75 us
    ppermute x2, starting transfers between devices, hook(): lax.ppermute(msg, 'dom', [p for p in far_pairs if p[0] % 4 in sides])  1.38 us
    dynamic_slice x1, local copies, waits for them, and re-layouts, body(): lax.dynamic_slice_in_dim(features, jnp.where(odd, 0, rows - width), width...  1.28 us
  transfers between devices with their start and end apart: 11, of which 5 were waited for; matrix products, arithmetic and copies ran while one was open for 0% of the time, Pallas kernels for 32%

profile of v3, /device:TPU:0, one launch (start us, length us, event | category | flops | bytes accessed | tf_op | source)
XLA Modules:
  0.0 53.9 jit_solution(14631221400222402782)
XLA Ops:
  0.7 1.3 %constant_dynamic-slice_fusion = (bf16[2,512,256]{2,1,0:T(8,128)(2,1)S(1)}, bf16[2,512,256]{2,1,0:T(8,128)(2,1)S(1)}) fusion(bf16[2,2048,256]{2,1,0:T(8,128)(2,1)} %x_hbm.1, s32[]{:T(128)S(6)} %select_n.10, s32[]{:T(128)S(6)} %select_n.9), kind=kLoop, calls=%fused_computation | loop fusion | bytes 2097160 | tf_op jit(solution)/shard_map/dynamic_slice | solution.py:375
  1.9 0.5 collective-permute-start.1
  2.5 0.7 %collective-permute-start = (bf16[2,512,256]{2,1,0:T(8,128)(2,1)S(1)}, bf16[2,512,256]{2,1,0:T(8,128)(2,1)S(1)}, u32[]{:S(2)}, u32[]{:S(2)}) collective-permute-start(bf16[2,512,256]{2,1,0:T(8,128)(2,1)S(1)} %get-tuple-element.92), channel_id=1, source_target_pairs={{1,2},{2,1},{3,4},{4,3},{5,6},{6,5},{7,8},{8,7},{9,10},{10,9},{11,... | collective-permute-start | bytes 1572872 | tf_op jit(solution)/shard_map/ppermute | solution.py:374
  3.2 8.9 %mid_rows.1 = (bf16[2,2048,256]{2,1,0:T(8,128)(2,1)}, bf16[2,3072,256]{2,1,0:T(8,128)(2,1)S(1)}, f32[2,3072,256]{2,1,0:T(8,128)S(1)}, f32[768,256]{1,0:T(8,128)S...) custom-call(s32[1]{0:T(128)} %bitcast.idx, ...), custom_call_target="tpu_custom_call" | custom-call | flops 1 | tf_op jit(solution)/shard_map/mid_rows/pallas_call | solution.py:390
  12.1 4.1 %near_rows.1 = (bf16[2,2048,256]{2,1,0:T(8,128)(2,1)}, bf16[2,3072,256]{2,1,0:T(8,128)(2,1)S(1)}, f32[2,3072,256]{2,1,0:T(8,128)S(1)}, f32[768,256]{1,0:T(8,128)S(1)}, bf16[2,512,256]{2,1,0:T(8,128)(2,1)S(1)}) custom-call(s32[1]{0:T(128)} %bitcast.idx, ...), custom_call_target="tpu_custom_call", output_to_operand_aliasing={{0}: (9, {}), {1}: (10, {}), {2}: (11, {}), {3}: (12, {})} | custom-call | flops 1 | tf_op jit(solution)/shard_map/near_rows/pallas_call | solution.py:390
  16.2 2.4 %far_rows.1 = (bf16[2,3072,256]{2,1,0:T(8,128)(2,1)S(1)}, f32[384,256]{1,0:T(8,128)S(1)}, f32[384,256]{1,0:T(8,128)S(1)}, bf16[2,512,256]{2,1,0:T(8,128)(2,1)S(1...) custom-call(s32[1]{0:T(128)} %bitcast.idx, ...), custom_call_target="tpu_custom_call", output_to_operand_aliasing={{0}: (9, {})} | custom-call | flops 1 | tf_op jit(solution)/shard_map/far_rows/pallas_call | solution.py:390
  18.6 3.9 %collective-permute-start.2 = (f32[384,256]{1,0:T(8,128)S(1)}, f32[384,256]{1,0:T(8,128)S(1)}, u32[]{:S(2)}, u32[]{:S(2)}) collective-permute-start(f32[384,256]{1,0:T(8,128)S(1)} %get-tuple-element.62), channel_id=1, source_target_pairs={{0,1},{1,0},{2,3},{3,2},{4,5},{5,4},{6,7},{7,6},{8,9},{9,8},{10,11... | collective-permute-start | bytes 1179656 | tf_op jit(solution)/shard_map/ppermute | solution.py:283
  22.6 0.1 collective-permute-start.4
  22.7 1.5 %messages.1 = (f32[2,3072,256]{2,1,0:T(8,128)S(1)}, bf16[2,512,256]{2,1,0:T(8,128)(2,1)S(1)}) custom-call(s32[1]{0:T(128)} %bitcast.idx, s32[4,16]{1,0:T(4,128)S(1)} %bitcast.5, bf16[2,512,256]{2,1,0:T(8,128)(2,1)S(1)} %get-tuple-element.64.dpre, bf16[4,128,512]{2,1,0:T(8,128)(2,1)S(1)} %get-tuple-element.65.acat, ...), custom_call_target="tpu_custom_call", output_to_operand_aliasing={{0}: (5, {})} | custom-call | flops 1 | tf_op jit(solution)/shard_map/messages/pallas_call | solution.py:390
  24.2 1.9 %collective-permute-start.3 = (bf16[192,256]{1,0:T(8,128)(2,1)S(1)}, bf16[192,256]{1,0:T(8,128)(2,1)S(1)}, u32[]{:S(2)}, u32[]{:S(2)}) collective-permute-start(bf16[192,256]{1,0:T(8,128)(2,1)S(1)} %get-tuple-element.70), channel_id=1, source_target_pairs={{0,4},{1,5},{2,6},{3,7},{4,0},{5,1},{6,2},{7,3},{8,12},{9,13},{10,... | collective-permute-start | bytes 294920 | tf_op jit(solution)/shard_map/ppermute | solution.py:283
  26.2 0.7 %collective-permute-start.8 = (bf16[2,512,256]{2,1,0:T(8,128)(2,1)S(1)}, bf16[2,512,256]{2,1,0:T(8,128)(2,1)S(1)}, u32[]{:S(2)}, u32[]{:S(2)}) collective-permute-start(bf16[2,512,256]{2,1,0:T(8,128)(2,1)S(1)} %get-tuple-element.84), channel_id=1, source_target_pairs={{3,4},{4,3},{7,8},{8,7},{11,12},{12,11},{19,20},{20,19},{23,24},{2... | collective-permute-start | bytes 1572872 | tf_op jit(solution)/shard_map/ppermute | solution.py:460
  26.9 2.6 %collective-permute-done.3.other = bf16[192,256]{1,0:T(8,128)(2,1)S(1)} collective-permute-done((bf16[192,256]{1,0:T(8,128)(2,1)S(1)}, bf16[192,256]{1,0:T(8,128)(2,1)S(1)}, u32[]{:S(2)}, u32[]{:S(2)}) %collective-permute-start.3) | collective-permute-done | bytes 98336 | tf_op jit(solution)/shard_map/ppermute | solution.py:283
  29.5 0.7 %collective-permute-start.7 = (bf16[2,512,256]{2,1,0:T(8,128)(2,1)S(1)}, bf16[2,512,256]{2,1,0:T(8,128)(2,1)S(1)}, u32[]{:S(2)}, u32[]{:S(2)}) collective-permute-start(bf16[2,512,256]{2,1,0:T(8,128)(2,1)S(1)} %get-tuple-element.84), channel_id=1, source_target_pairs={{1,2},{2,1},{5,6},{6,5},{9,10},{10,9},{13,14},{14,13},{17,18},{18,... | collective-permute-start | bytes 1572872 | tf_op jit(solution)/shard_map/ppermute | solution.py:460
  30.2 2.7 %collective-permute-start.5 = (bf16[192,256]{1,0:T(8,128)(2,1)S(1)}, bf16[192,256]{1,0:T(8,128)(2,1)S(1)}, u32[]{:S(2)}, u32[]{:S(2)}) collective-permute-start(bf16[192,256]{1,0:T(8,128)(2,1)S(1)} %add.5.mine), channel_id=1, source_target_pairs={{0,8},{1,9},{2,10},{3,11},{4,12},{5,13},{6,14},{7,15},{8,0},{9,1},... | collective-permute-start | bytes 294920 | tf_op jit(solution)/shard_map/ppermute | solution.py:283
  32.8 1.9 %own_rows.1 = (bf16[2,2048,256]{2,1,0:T(8,128)(2,1)}, bf16[2,2048,256]{2,1,0:T(8,128)(2,1)}, f32[2,512,256]{2,1,0:T(8,128)S(1)}) custom-call(s32[1]{0:T(128)} %bitcast.idx, bf16[2,512,256]{2,1,0:T(8,128)(2,1)S(1)} %collective-permute-done.4.nrecv, bf16[2,512,256]{2,1,0:T(8,128)(2,1)S(1)} %get-tuple-element.73.act, ...), custom_call_target="tpu_custom_call", output_to_operand_aliasing={{0}: (9, {})} | custom-call | flops 1 | tf_op jit(solution)/shard_map/own_rows/pallas_call | solution.py:390
  34.8 7.3 %collective-permute-done.5.other = bf16[192,256]{1,0:T(8,128)(2,1)S(1)} collective-permute-done((bf16[192,256]{1,0:T(8,128)(2,1)S(1)}, bf16[192,256]{1,0:T(8,128)(2,1)S(1)}, u32[]{:S(2)}, u32[]{:S(2)}) %collective-permute-start.5) | collective-permute-done | bytes 98336 | tf_op jit(solution)/shard_map/ppermute | solution.py:283
  42.1 0.1 collective-permute-start.6
  42.1 4.6 %collective-permute-done.6.other = bf16[192,256]{1,0:T(8,128)(2,1)S(1)} collective-permute-done((bf16[192,256]{1,0:T(8,128)(2,1)S(1)}, bf16[192,256]{1,0:T(8,128)(2,1)S(1)}, u32[]{:S(2)}, u32[]{:S(2)}) %collective-permute-start.6) | collective-permute-done | bytes 98336 | tf_op jit(solution)/shard_map/ppermute | solution.py:283
  46.8 0.1 collective-permute-start.9
  46.9 1.0 %edge_rows.1 = bf16[2,2048,256]{2,1,0:T(8,128)(2,1)} custom-call(s32[1]{0:T(128)} %bitcast.idx, f32[2,512,256]{2,1,0:T(8,128)S(1)} %get-tuple-element.81.edge_ref, bf16[2,512,256]{2,1,0:T(8,128)(2,1)S(1)} %collective-permute-done.7.straight_ref, bf16[2,512,256]{2,1,0:T(8,128)(2,1)S(1)} %collective-permute-done.8.across_ref, ...), custom_call_target="tpu_custom_call", output_to_operand_aliasing={{}: (4, {})} | custom-call | flops 1 | tf_op jit(solution)/shard_map/edge_rows/pallas_call | solution.py:390
  47.9 3.6 %collective-permute-done.9.other = bf16[192,256]{1,0:T(8,128)(2,1)S(1)} collective-permute-done((bf16[192,256]{1,0:T(8,128)(2,1)S(1)}, bf16[192,256]{1,0:T(8,128)(2,1)S(1)}, u32[]{:S(2)}, u32[]{:S(2)}) %collective-permute-start.9) | collective-permute-done | bytes 98336 | tf_op jit(solution)/shard_map/ppermute | solution.py:283
  51.5 0.1 collective-permute-start.10
  51.6 1.4 %collective-permute-done.10.other = bf16[384,256]{1,0:T(8,128)(2,1)S(1)} collective-permute-done((bf16[384,256]{1,0:T(8,128)(2,1)S(1)}, bf16[384,256]{1,0:T(8,128)(2,1)S(1)}, u32[]{:S(2)}, u32[]{:S(2)}) %collective-permute-start.10) | collective-permute-done | bytes 196640 | tf_op jit(solution)/shard_map/ppermute | solution.py:283
  53.0 0.9 %final.1 = (f32[256,256]{1,0:T(8,128)}, f32[256,256]{1,0:T(8,128)}, f32[256,256]{1,0:T(8,128)}) custom-call(s32[1]{0:T(128)} %bitcast.idx, bf16[384,256]{1,0:T(8,128)(2,1)S(1)} %join.1.mine, bf16[384,256]{1,0:T(8,128)(2,1)S(1)} %collective-permute-done.10.other), custom_call_target="tpu_custom_call" | custom-call | flops 1 | tf_op jit(solution)/shard_map/final/pallas_call | solution.py:390
  (15 shorter events, 0.2 us)
Async XLA Ops:
  0.6 2.5 %copy-start.1 = (s32[16]{0:T(128)S(1)}, s32[16]{0:T(128)}, u32[]{:S(2)}) copy-start(s32[16]{0:T(128)} %cnt_ref.5) | copy-start | bytes 196
  0.6 2.5 %copy-start = (s32[16,4]{0,1:T(4,128)S(1)}, s32[16,4]{0,1:T(4,128)}, u32[]{:S(2)}) copy-start(s32[16,4]{0,1:T(4,128)} %param.11) | copy-start | bytes 772
  1.9 10.1 %collective-permute-start.1 = (bf16[2,512,256]{2,1,0:T(8,128)(2,1)S(1)}, bf16[2,512,256]{2,1,0:T(8,128)(2,1)S(1)}, u32[]{:S(2)}, u32[]{:S(2)}) collective-permute-start(bf16[2,512,256]{2,1,0:T(8,128)(2,1)S(1)} %get-tuple-element.91), channel_id=1, source_target_pairs={{0,1},{1,0},{2,3},{3,2},{4,5},{5,4},{6,7},{7,6},{8,9},{9,8},{10,11... | collective-permute-start | bytes 1572872 | tf_op jit(solution)/shard_map/ppermute | solution.py:376
  2.5 13.7 %collective-permute-start = (bf16[2,512,256]{2,1,0:T(8,128)(2,1)S(1)}, bf16[2,512,256]{2,1,0:T(8,128)(2,1)S(1)}, u32[]{:S(2)}, u32[]{:S(2)}) collective-permute-start(bf16[2,512,256]{2,1,0:T(8,128)(2,1)S(1)} %get-tuple-element.92), channel_id=1, source_target_pairs={{1,2},{2,1},{3,4},{4,3},{5,6},{6,5},{7,8},{8,7},{9,10},{10,9},{11,... | collective-permute-start | bytes 1572872 | tf_op jit(solution)/shard_map/ppermute | solution.py:374
  18.6 5.5 %collective-permute-start.2 = (f32[384,256]{1,0:T(8,128)S(1)}, f32[384,256]{1,0:T(8,128)S(1)}, u32[]{:S(2)}, u32[]{:S(2)}) collective-permute-start(f32[384,256]{1,0:T(8,128)S(1)} %get-tuple-element.62), channel_id=1, source_target_pairs={{0,1},{1,0},{2,3},{3,2},{4,5},{5,4},{6,7},{7,6},{8,9},{9,8},{10,11... | collective-permute-start | bytes 1179656 | tf_op jit(solution)/shard_map/ppermute | solution.py:283
  22.6 10.3 %collective-permute-start.4 = (bf16[2,512,256]{2,1,0:T(8,128)(2,1)S(1)}, bf16[2,512,256]{2,1,0:T(8,128)(2,1)S(1)}, u32[]{:S(2)}, u32[]{:S(2)}) collective-permute-start(bf16[2,512,256]{2,1,0:T(8,128)(2,1)S(1)} %get-tuple-element.72), channel_id=1, source_target_pairs={{0,1},{1,0},{2,3},{3,2},{4,5},{5,4},{6,7},{7,6},{8,9},{9,8},{10,11... | collective-permute-start | bytes 1572872 | tf_op jit(solution)/shard_map/ppermute | solution.py:427
  24.2 5.2 %collective-permute-start.3 = (bf16[192,256]{1,0:T(8,128)(2,1)S(1)}, bf16[192,256]{1,0:T(8,128)(2,1)S(1)}, u32[]{:S(2)}, u32[]{:S(2)}) collective-permute-start(bf16[192,256]{1,0:T(8,128)(2,1)S(1)} %get-tuple-element.70), channel_id=1, source_target_pairs={{0,4},{1,5},{2,6},{3,7},{4,0},{5,1},{6,2},{7,3},{8,12},{9,13},{10,... | collective-permute-start | bytes 294920 | tf_op jit(solution)/shard_map/ppermute | solution.py:283
  26.2 20.7 %collective-permute-start.8 = (bf16[2,512,256]{2,1,0:T(8,128)(2,1)S(1)}, bf16[2,512,256]{2,1,0:T(8,128)(2,1)S(1)}, u32[]{:S(2)}, u32[]{:S(2)}) collective-permute-start(bf16[2,512,256]{2,1,0:T(8,128)(2,1)S(1)} %get-tuple-element.84), channel_id=1, source_target_pairs={{3,4},{4,3},{7,8},{8,7},{11,12},{12,11},{19,20},{20,19},{23,24},{2... | collective-permute-start | bytes 1572872 | tf_op jit(solution)/shard_map/ppermute | solution.py:460
  29.5 17.4 %collective-permute-start.7 = (bf16[2,512,256]{2,1,0:T(8,128)(2,1)S(1)}, bf16[2,512,256]{2,1,0:T(8,128)(2,1)S(1)}, u32[]{:S(2)}, u32[]{:S(2)}) collective-permute-start(bf16[2,512,256]{2,1,0:T(8,128)(2,1)S(1)} %get-tuple-element.84), channel_id=1, source_target_pairs={{1,2},{2,1},{5,6},{6,5},{9,10},{10,9},{13,14},{14,13},{17,18},{18,... | collective-permute-start | bytes 1572872 | tf_op jit(solution)/shard_map/ppermute | solution.py:460
  30.2 11.9 %collective-permute-start.5 = (bf16[192,256]{1,0:T(8,128)(2,1)S(1)}, bf16[192,256]{1,0:T(8,128)(2,1)S(1)}, u32[]{:S(2)}, u32[]{:S(2)}) collective-permute-start(bf16[192,256]{1,0:T(8,128)(2,1)S(1)} %add.5.mine), channel_id=1, source_target_pairs={{0,8},{1,9},{2,10},{3,11},{4,12},{5,13},{6,14},{7,15},{8,0},{9,1},... | collective-permute-start | bytes 294920 | tf_op jit(solution)/shard_map/ppermute | solution.py:283
  42.1 4.7 %collective-permute-start.6 = (bf16[192,256]{1,0:T(8,128)(2,1)S(1)}, bf16[192,256]{1,0:T(8,128)(2,1)S(1)}, u32[]{:S(2)}, u32[]{:S(2)}) collective-permute-start(bf16[192,256]{1,0:T(8,128)(2,1)S(1)} %add.6.mine), channel_id=1, source_target_pairs={{0,2},{1,3},{2,0},{3,1},{4,6},{5,7},{6,4},{7,5},{8,10},{9,11},{10,... | collective-permute-start | bytes 294920 | tf_op jit(solution)/shard_map/ppermute | solution.py:283
  46.8 4.7 %collective-permute-start.9 = (bf16[192,256]{1,0:T(8,128)(2,1)S(1)}, bf16[192,256]{1,0:T(8,128)(2,1)S(1)}, u32[]{:S(2)}, u32[]{:S(2)}) collective-permute-start(bf16[192,256]{1,0:T(8,128)(2,1)S(1)} %add.7.mine), channel_id=1, source_target_pairs={{0,4},{1,5},{2,6},{3,7},{4,0},{5,1},{6,2},{7,3},{8,12},{9,13},{10,... | collective-permute-start | bytes 294920 | tf_op jit(solution)/shard_map/ppermute | solution.py:283
  51.5 1.5 %collective-permute-start.10 = (bf16[384,256]{1,0:T(8,128)(2,1)S(1)}, bf16[384,256]{1,0:T(8,128)(2,1)S(1)}, u32[]{:S(2)}, u32[]{:S(2)}) collective-permute-start(bf16[384,256]{1,0:T(8,128)(2,1)S(1)} %join.1.mine), channel_id=1, source_target_pairs={{0,1},{1,0},{2,3},{3,2},{4,5},{5,4},{6,7},{7,6},{8,9},{9,8},{10,11... | collective-permute-start | bytes 589832 | tf_op jit(solution)/shard_map/ppermute | solution.py:283

commit v4 on v3

--- a/solution.py
+++ b/solution.py
@@ -14,7 +14,7 @@
 ANY = pl.BlockSpec(memory_space=pltpu.HBM)
 VM = pl.BlockSpec(memory_space=pltpu.VMEM)
 SM = pl.BlockSpec(memory_space=pltpu.SMEM)
-OWN_AT, EDGE_AT = 2, 4
+OWN_AT, EDGE_AT = 2, 3
 COSTS = dict(mid_rows=1, near_rows=1, far_rows=1, messages=1, own_rows=1, edge_rows=1)
 LIMIT = 12 * 1024 * 1024
 
@@ -299,8 +299,11 @@
     keep_ref[...] = mine[stay, :] + other[stay, :].astype(F32)
 
 
-def add_kernel(mine, other, out_ref):
-    out_ref[...] = (mine[...].astype(F32) + other[...].astype(F32)).astype(BF16)
+def add_kernel(*refs):
+    values = [ref[...].astype(F32) for ref in refs[:-1]]
+    while len(values) > 1:
+        values = [a + b for a, b in zip(values[::2], values[1::2])]
+    refs[-1][...] = values[0].astype(BF16)
 
 
 def join_kernel(shift, idx, mine, other, out_ref):
@@ -309,11 +312,15 @@
     out_ref[half_rows(out_ref, 1 - bit), :] = other[...]
 
 
-def final_kernel(factor, idx, mine, other, gs_ref, gn_ref, go_ref, all_s):
+def final_kernel(factor, idx, mine, other, gs_hbm, gn_hbm, go_hbm, all_s, out_s, sems):
     join_kernel(0, idx, mine, other, all_s)
-    hidden = gs_ref.shape[0]
-    for p, ref in enumerate((gs_ref, gn_ref, go_ref)):
-        ref[...] = all_s[p * hidden : (p + 1) * hidden, :].astype(F32) * factor
+    hidden = gs_hbm.shape[0]
+    copies = []
+    for p, ref in enumerate((gs_hbm, gn_hbm, go_hbm)):
+        out_s[p] = all_s[p * hidden : (p + 1) * hidden, :].astype(F32) * factor
+        copies.append(pltpu.make_async_copy(out_s.at[p], ref, sems.at[p]))
+        copies[-1].start()
+    wait_all(copies)
 
 
 def reduce_all(call, keep, send, idx, factor, hooks):
@@ -341,10 +348,18 @@
             [SM, VM, VM], (vm(rows, F32), vm(rows, BF16)), (VM, VM), [],
         )
         other = exchange(out, shift)
-    for shift in [None] + [s for s in reversed(shifts) if s not in scatter]:
-        if shift is not None:
-            other = exchange(mine, shift)
-        mine = call(add_kernel, "add", (mine, other), [VM, VM], vm(mine.shape[0], BF16), VM, [])
+    mine = call(add_kernel, "add", (mine, other), [VM, VM], vm(mine.shape[0], BF16), VM, [])
+    rest = [s for s in reversed(shifts) if s not in scatter]
+    while rest:
+        group, rest = rest[:2], rest[2:]
+        masks = [1 << s for s in group]
+        if len(masks) == 2:
+            masks.append(masks[0] | masks[1])
+        moved = [swap(mine, mask) for mask in masks]
+        for hook in hooks.get(next(stage), ()):
+            moved = hook(mine, moved)
+        parts = (mine, *(in_vmem(part) for part in moved))
+        mine = call(add_kernel, "add", parts, [VM] * len(parts), vm(mine.shape[0], BF16), VM, [])
     for shift in reversed(scatter):
         other = exchange(mine, shift)
         mine = call(
@@ -354,7 +369,8 @@
     other = exchange(mine, 0)
     return call(
         functools.partial(final_kernel, factor), "final", (idx, mine, other),
-        [SM, VM, VM], (sds((hidden, hidden), F32),) * 3, (VM,) * 3, [vm(3 * hidden, BF16)],
+        [SM, VM, VM], (sds((hidden, hidden), F32),) * 3, (ANY,) * 3,
+        [vm(3 * hidden, BF16), pltpu.VMEM((3, hidden, hidden), F32), pltpu.SemaphoreType.DMA((3,))],
     )
 
 
@@ -491,7 +507,7 @@
         return before
 
     factor = 1.0 / math.sqrt(2.0 * rows * count)
-    hooks = {0: (message, send_far("across", (0, 3)),), 2: (send_far("straight", (1, 2)),)}
+    hooks = {0: (message, send_far("across", (0, 3))), 2: (send_far("straight", (1, 2)),)}
     for at, hook in ((OWN_AT, own), (EDGE_AT, edge)):
         hooks[at] = hooks.get(at, ()) + (hook,)
     sums = reduce_all(call, keep, send, idx, factor, hooks)

time: 54.1 us -> 54.1 us (level)
  starting transfers between devices: 11.4 us -> 15.5 us
  waiting for transfers between devices: 19.5 us -> 15.5 us
    ppermute x6 -> x7, starting transfers between devices: 8.75 us -> 12.8 us  [swap(): return lax.ppermute(value, 'dom', [(i, i ^ bit) for i in range(count)])]
    ppermute x6 -> x7, waiting for transfers between devices: 19.5 us -> 15.4 us  [swap(): return lax.ppermute(value, 'dom', [(i, i ^ bit) for i in range(count)])]
    pallas_call x12 -> x11, Pallas kernels: 20.9 us -> 20.9 us  [call(): pl.pallas_call(kernel, out_shape=outs, in_specs=in_specs, out_specs=out_s...]
  transfers between devices with their start and end apart: 11 -> 12, of which waited for: 5 -> 6; matrix products, arithmetic and copies ran while one was open for 0% -> 0% of each run, Pallas kernels for 32% -> 32%
where the time goes in v4:
time: 54.1 us; the launch traced here: 53.9 us
  Pallas kernels  20.9 us (39%)
  starting transfers between devices  15.5 us (29%)
  waiting for transfers between devices  15.5 us (29%)
  local copies, waits for them, and re-layouts  1.29 us (2%)
  between operations  0.8 us (1%)
    pallas_call x11, Pallas kernels, call(): pl.pallas_call(kernel, out_shape=outs, in_specs=in_specs, out_specs=out_s...  20.9 us
    ppermute x7, waiting for transfers between devices, swap(): return lax.ppermute(value, 'dom', [(i, i ^ bit) for i in range(count)])  15.4 us
    ppermute x7, starting transfers between devices, swap(): return lax.ppermute(value, 'dom', [(i, i ^ bit) for i in range(count)])  12.8 us
    ppermute x2, starting transfers between devices, hook(): lax.ppermute(msg, 'dom', [p for p in far_pairs if p[0] % 4 in sides])  1.38 us
    dynamic_slice x1, local copies, waits for them, and re-layouts, body(): lax.dynamic_slice_in_dim(features, jnp.where(odd, 0, rows - width), width...  1.28 us
  transfers between devices with their start and end apart: 12, of which 6 were waited for; matrix products, arithmetic and copies ran while one was open for 0% of the time, Pallas kernels for 32%

profile of v4, /device:TPU:0, one launch (start us, length us, event | category | flops | bytes accessed | tf_op | source)
XLA Modules:
  0.0 53.9 jit_solution(6754377160597377490)
XLA Ops:
  0.7 1.3 %constant_dynamic-slice_fusion = (bf16[2,512,256]{2,1,0:T(8,128)(2,1)S(1)}, bf16[2,512,256]{2,1,0:T(8,128)(2,1)S(1)}) fusion(bf16[2,2048,256]{2,1,0:T(8,128)(2,1)} %x_hbm.1, s32[]{:T(128)S(6)} %select_n.10, s32[]{:T(128)S(6)} %select_n.9), kind=kLoop, calls=%fused_computation | loop fusion | bytes 2097160 | tf_op jit(solution)/shard_map/dynamic_slice | solution.py:391
  1.9 0.5 collective-permute-start.1
  2.5 0.7 %collective-permute-start = (bf16[2,512,256]{2,1,0:T(8,128)(2,1)S(1)}, bf16[2,512,256]{2,1,0:T(8,128)(2,1)S(1)}, u32[]{:S(2)}, u32[]{:S(2)}) collective-permute-start(bf16[2,512,256]{2,1,0:T(8,128)(2,1)S(1)} %get-tuple-element.96), channel_id=1, source_target_pairs={{1,2},{2,1},{3,4},{4,3},{5,6},{6,5},{7,8},{8,7},{9,10},{10,9},{11,... | collective-permute-start | bytes 1572872 | tf_op jit(solution)/shard_map/ppermute | solution.py:390
  3.2 8.9 %mid_rows.1 = (bf16[2,2048,256]{2,1,0:T(8,128)(2,1)}, bf16[2,3072,256]{2,1,0:T(8,128)(2,1)S(1)}, f32[2,3072,256]{2,1,0:T(8,128)S(1)}, f32[768,256]{1,0:T(8,128)S...) custom-call(s32[1]{0:T(128)} %bitcast.idx, ...), custom_call_target="tpu_custom_call" | custom-call | flops 1 | tf_op jit(solution)/shard_map/mid_rows/pallas_call | solution.py:406
  12.1 4.1 %near_rows.1 = (bf16[2,2048,256]{2,1,0:T(8,128)(2,1)}, bf16[2,3072,256]{2,1,0:T(8,128)(2,1)S(1)}, f32[2,3072,256]{2,1,0:T(8,128)S(1)}, f32[768,256]{1,0:T(8,128)S(1)}, bf16[2,512,256]{2,1,0:T(8,128)(2,1)S(1)}) custom-call(s32[1]{0:T(128)} %bitcast.idx, ...), custom_call_target="tpu_custom_call", output_to_operand_aliasing={{0}: (9, {}), {1}: (10, {}), {2}: (11, {}), {3}: (12, {})} | custom-call | flops 1 | tf_op jit(solution)/shard_map/near_rows/pallas_call | solution.py:406
  16.2 2.4 %far_rows.1 = (bf16[2,3072,256]{2,1,0:T(8,128)(2,1)S(1)}, f32[384,256]{1,0:T(8,128)S(1)}, f32[384,256]{1,0:T(8,128)S(1)}, bf16[2,512,256]{2,1,0:T(8,128)(2,1)S(1...) custom-call(s32[1]{0:T(128)} %bitcast.idx, ...), custom_call_target="tpu_custom_call", output_to_operand_aliasing={{0}: (9, {})} | custom-call | flops 1 | tf_op jit(solution)/shard_map/far_rows/pallas_call | solution.py:406
  18.6 3.9 %collective-permute-start.2 = (f32[384,256]{1,0:T(8,128)S(1)}, f32[384,256]{1,0:T(8,128)S(1)}, u32[]{:S(2)}, u32[]{:S(2)}) collective-permute-start(f32[384,256]{1,0:T(8,128)S(1)} %get-tuple-element.64), channel_id=1, source_target_pairs={{0,1},{1,0},{2,3},{3,2},{4,5},{5,4},{6,7},{7,6},{8,9},{9,8},{10,11... | collective-permute-start | bytes 1179656 | tf_op jit(solution)/shard_map/ppermute | solution.py:283
  22.6 0.1 collective-permute-start.4
  22.7 1.5 %messages.1 = (f32[2,3072,256]{2,1,0:T(8,128)S(1)}, bf16[2,512,256]{2,1,0:T(8,128)(2,1)S(1)}) custom-call(s32[1]{0:T(128)} %bitcast.idx, s32[4,16]{1,0:T(4,128)S(1)} %bitcast.5, bf16[2,512,256]{2,1,0:T(8,128)(2,1)S(1)} %get-tuple-element.66.dpre, bf16[4,128,512]{2,1,0:T(8,128)(2,1)S(1)} %get-tuple-element.67.acat, ...), custom_call_target="tpu_custom_call", output_to_operand_aliasing={{0}: (5, {})} | custom-call | flops 1 | tf_op jit(solution)/shard_map/messages/pallas_call | solution.py:406
  24.2 1.9 %collective-permute-start.3 = (bf16[192,256]{1,0:T(8,128)(2,1)S(1)}, bf16[192,256]{1,0:T(8,128)(2,1)S(1)}, u32[]{:S(2)}, u32[]{:S(2)}) collective-permute-start(bf16[192,256]{1,0:T(8,128)(2,1)S(1)} %get-tuple-element.72), channel_id=1, source_target_pairs={{0,4},{1,5},{2,6},{3,7},{4,0},{5,1},{6,2},{7,3},{8,12},{9,13},{10,... | collective-permute-start | bytes 294920 | tf_op jit(solution)/shard_map/ppermute | solution.py:283
  26.2 0.7 %collective-permute-start.9 = (bf16[2,512,256]{2,1,0:T(8,128)(2,1)S(1)}, bf16[2,512,256]{2,1,0:T(8,128)(2,1)S(1)}, u32[]{:S(2)}, u32[]{:S(2)}) collective-permute-start(bf16[2,512,256]{2,1,0:T(8,128)(2,1)S(1)} %get-tuple-element.88), channel_id=1, source_target_pairs={{3,4},{4,3},{7,8},{8,7},{11,12},{12,11},{19,20},{20,19},{23,24},{2... | collective-permute-start | bytes 1572872 | tf_op jit(solution)/shard_map/ppermute | solution.py:476
  26.9 2.6 %collective-permute-done.3.refs_1_ = bf16[192,256]{1,0:T(8,128)(2,1)S(1)} collective-permute-done((bf16[192,256]{1,0:T(8,128)(2,1)S(1)}, bf16[192,256]{1,0:T(8,128)(2,1)S(1)}, u32[]{:S(2)}, u32[]{:S(2)}) %collective-permute-start.3) | collective-permute-done | bytes 98336 | tf_op jit(solution)/shard_map/ppermute | solution.py:283
  29.5 0.7 %collective-permute-start.8 = (bf16[2,512,256]{2,1,0:T(8,128)(2,1)S(1)}, bf16[2,512,256]{2,1,0:T(8,128)(2,1)S(1)}, u32[]{:S(2)}, u32[]{:S(2)}) collective-permute-start(bf16[2,512,256]{2,1,0:T(8,128)(2,1)S(1)} %get-tuple-element.88), channel_id=1, source_target_pairs={{1,2},{2,1},{5,6},{6,5},{9,10},{10,9},{13,14},{14,13},{17,18},{18,... | collective-permute-start | bytes 1572872 | tf_op jit(solution)/shard_map/ppermute | solution.py:476
  30.2 4.8 %collective-permute-start.7 = (bf16[192,256]{1,0:T(8,128)(2,1)S(1)}, bf16[192,256]{1,0:T(8,128)(2,1)S(1)}, u32[]{:S(2)}, u32[]{:S(2)}) collective-permute-start(bf16[192,256]{1,0:T(8,128)(2,1)S(1)} %add.4.refs_0_), channel_id=1, source_target_pairs={{0,10},{1,11},{2,8},{3,9},{4,14},{5,15},{6,12},{7,13},{8,2},{9,3},... | collective-permute-start | bytes 294920 | tf_op jit(solution)/shard_map/ppermute | solution.py:283
  35.0 0.6 %collective-permute-start.5 = (bf16[192,256]{1,0:T(8,128)(2,1)S(1)}, bf16[192,256]{1,0:T(8,128)(2,1)S(1)}, u32[]{:S(2)}, u32[]{:S(2)}) collective-permute-start(bf16[192,256]{1,0:T(8,128)(2,1)S(1)} %add.4.refs_0_), channel_id=1, source_target_pairs={{0,8},{1,9},{2,10},{3,11},{4,12},{5,13},{6,14},{7,15},{8,0},{9,1},... | collective-permute-start | bytes 294920 | tf_op jit(solution)/shard_map/ppermute | solution.py:283
  35.7 1.9 %own_rows.1 = (bf16[2,2048,256]{2,1,0:T(8,128)(2,1)}, bf16[2,2048,256]{2,1,0:T(8,128)(2,1)}, f32[2,512,256]{2,1,0:T(8,128)S(1)}) custom-call(s32[1]{0:T(128)} %bitcast.idx, bf16[2,512,256]{2,1,0:T(8,128)(2,1)S(1)} %collective-permute-done.4.nrecv, bf16[2,512,256]{2,1,0:T(8,128)(2,1)S(1)} %get-tuple-element.75.act, ...), custom_call_target="tpu_custom_call", output_to_operand_aliasing={{0}: (9, {})} | custom-call | flops 1 | tf_op jit(solution)/shard_map/own_rows/pallas_call | solution.py:406
  37.6 3.8 %collective-permute-done.7.refs_3_ = bf16[192,256]{1,0:T(8,128)(2,1)S(1)} collective-permute-done((bf16[192,256]{1,0:T(8,128)(2,1)S(1)}, bf16[192,256]{1,0:T(8,128)(2,1)S(1)}, u32[]{:S(2)}, u32[]{:S(2)}) %collective-permute-start.7) | collective-permute-done | bytes 98336 | tf_op jit(solution)/shard_map/ppermute | solution.py:283
  41.4 2.9 %collective-permute-done.6.refs_2_ = bf16[192,256]{1,0:T(8,128)(2,1)S(1)} collective-permute-done((bf16[192,256]{1,0:T(8,128)(2,1)S(1)}, bf16[192,256]{1,0:T(8,128)(2,1)S(1)}, u32[]{:S(2)}, u32[]{:S(2)}) %collective-permute-start.6) | collective-permute-done | bytes 98336 | tf_op jit(solution)/shard_map/ppermute | solution.py:283
  44.3 2.0 %collective-permute-done.5.refs_1_ = bf16[192,256]{1,0:T(8,128)(2,1)S(1)} collective-permute-done((bf16[192,256]{1,0:T(8,128)(2,1)S(1)}, bf16[192,256]{1,0:T(8,128)(2,1)S(1)}, u32[]{:S(2)}, u32[]{:S(2)}) %collective-permute-start.5) | collective-permute-done | bytes 98336 | tf_op jit(solution)/shard_map/ppermute | solution.py:283
  46.3 1.4 %collective-permute-start.10 = (bf16[192,256]{1,0:T(8,128)(2,1)S(1)}, bf16[192,256]{1,0:T(8,128)(2,1)S(1)}, u32[]{:S(2)}, u32[]{:S(2)}) collective-permute-start(bf16[192,256]{1,0:T(8,128)(2,1)S(1)} %add.5.mine), channel_id=1, source_target_pairs={{0,4},{1,5},{2,6},{3,7},{4,0},{5,1},{6,2},{7,3},{8,12},{9,13},{10,... | collective-permute-start | bytes 294920 | tf_op jit(solution)/shard_map/ppermute | solution.py:283
  47.7 1.0 %edge_rows.1 = bf16[2,2048,256]{2,1,0:T(8,128)(2,1)} custom-call(s32[1]{0:T(128)} %bitcast.idx, f32[2,512,256]{2,1,0:T(8,128)S(1)} %get-tuple-element.85.edge_ref, bf16[2,512,256]{2,1,0:T(8,128)(2,1)S(1)} %collective-permute-done.8.straight_ref, bf16[2,512,256]{2,1,0:T(8,128)(2,1)S(1)} %collective-permute-done.9.across_ref, ...), custom_call_target="tpu_custom_call", output_to_operand_aliasing={{}: (4, {})} | custom-call | flops 1 | tf_op jit(solution)/shard_map/edge_rows/pallas_call | solution.py:406
  48.7 2.7 %collective-permute-done.10.other = bf16[192,256]{1,0:T(8,128)(2,1)S(1)} collective-permute-done((bf16[192,256]{1,0:T(8,128)(2,1)S(1)}, bf16[192,256]{1,0:T(8,128)(2,1)S(1)}, u32[]{:S(2)}, u32[]{:S(2)}) %collective-permute-start.10) | collective-permute-done | bytes 98336 | tf_op jit(solution)/shard_map/ppermute | solution.py:283
  51.5 1.4 %collective-permute-done.11.other = bf16[384,256]{1,0:T(8,128)(2,1)S(1)} collective-permute-done((bf16[384,256]{1,0:T(8,128)(2,1)S(1)}, bf16[384,256]{1,0:T(8,128)(2,1)S(1)}, u32[]{:S(2)}, u32[]{:S(2)}) %collective-permute-start.11) | collective-permute-done | bytes 196640 | tf_op jit(solution)/shard_map/ppermute | solution.py:283
  53.0 1.0 %final.1 = (f32[256,256]{1,0:T(8,128)}, f32[256,256]{1,0:T(8,128)}, f32[256,256]{1,0:T(8,128)}) custom-call(s32[1]{0:T(128)} %bitcast.idx, bf16[384,256]{1,0:T(8,128)(2,1)S(1)} %join.1.mine, bf16[384,256]{1,0:T(8,128)(2,1)S(1)} %collective-permute-done.11.other), custom_call_target="tpu_custom_call" | custom-call | flops 1 | tf_op jit(solution)/shard_map/final/pallas_call | solution.py:406
  (16 shorter events, 0.2 us)
Async XLA Ops:
  0.6 2.5 %copy-start.1 = (s32[16]{0:T(128)S(1)}, s32[16]{0:T(128)}, u32[]{:S(2)}) copy-start(s32[16]{0:T(128)} %cnt_ref.5) | copy-start | bytes 196
  0.6 2.5 %copy-start = (s32[16,4]{0,1:T(4,128)S(1)}, s32[16,4]{0,1:T(4,128)}, u32[]{:S(2)}) copy-start(s32[16,4]{0,1:T(4,128)} %param.11) | copy-start | bytes 772
  1.9 10.1 %collective-permute-start.1 = (bf16[2,512,256]{2,1,0:T(8,128)(2,1)S(1)}, bf16[2,512,256]{2,1,0:T(8,128)(2,1)S(1)}, u32[]{:S(2)}, u32[]{:S(2)}) collective-permute-start(bf16[2,512,256]{2,1,0:T(8,128)(2,1)S(1)} %get-tuple-element.95), channel_id=1, source_target_pairs={{0,1},{1,0},{2,3},{3,2},{4,5},{5,4},{6,7},{7,6},{8,9},{9,8},{10,11... | collective-permute-start | bytes 1572872 | tf_op jit(solution)/shard_map/ppermute | solution.py:392
  2.5 13.7 %collective-permute-start = (bf16[2,512,256]{2,1,0:T(8,128)(2,1)S(1)}, bf16[2,512,256]{2,1,0:T(8,128)(2,1)S(1)}, u32[]{:S(2)}, u32[]{:S(2)}) collective-permute-start(bf16[2,512,256]{2,1,0:T(8,128)(2,1)S(1)} %get-tuple-element.96), channel_id=1, source_target_pairs={{1,2},{2,1},{3,4},{4,3},{5,6},{6,5},{7,8},{8,7},{9,10},{10,9},{11,... | collective-permute-start | bytes 1572872 | tf_op jit(solution)/shard_map/ppermute | solution.py:390
  18.6 5.5 %collective-permute-start.2 = (f32[384,256]{1,0:T(8,128)S(1)}, f32[384,256]{1,0:T(8,128)S(1)}, u32[]{:S(2)}, u32[]{:S(2)}) collective-permute-start(f32[384,256]{1,0:T(8,128)S(1)} %get-tuple-element.64), channel_id=1, source_target_pairs={{0,1},{1,0},{2,3},{3,2},{4,5},{5,4},{6,7},{7,6},{8,9},{9,8},{10,11... | collective-permute-start | bytes 1179656 | tf_op jit(solution)/shard_map/ppermute | solution.py:283
  22.6 12.4 %collective-permute-start.4 = (bf16[2,512,256]{2,1,0:T(8,128)(2,1)S(1)}, bf16[2,512,256]{2,1,0:T(8,128)(2,1)S(1)}, u32[]{:S(2)}, u32[]{:S(2)}) collective-permute-start(bf16[2,512,256]{2,1,0:T(8,128)(2,1)S(1)} %get-tuple-element.74), channel_id=1, source_target_pairs={{0,1},{1,0},{2,3},{3,2},{4,5},{5,4},{6,7},{7,6},{8,9},{9,8},{10,11... | collective-permute-start | bytes 1572872 | tf_op jit(solution)/shard_map/ppermute | solution.py:443
  24.2 5.2 %collective-permute-start.3 = (bf16[192,256]{1,0:T(8,128)(2,1)S(1)}, bf16[192,256]{1,0:T(8,128)(2,1)S(1)}, u32[]{:S(2)}, u32[]{:S(2)}) collective-permute-start(bf16[192,256]{1,0:T(8,128)(2,1)S(1)} %get-tuple-element.72), channel_id=1, source_target_pairs={{0,4},{1,5},{2,6},{3,7},{4,0},{5,1},{6,2},{7,3},{8,12},{9,13},{10,... | collective-permute-start | bytes 294920 | tf_op jit(solution)/shard_map/ppermute | solution.py:283
  26.2 21.5 %collective-permute-start.9 = (bf16[2,512,256]{2,1,0:T(8,128)(2,1)S(1)}, bf16[2,512,256]{2,1,0:T(8,128)(2,1)S(1)}, u32[]{:S(2)}, u32[]{:S(2)}) collective-permute-start(bf16[2,512,256]{2,1,0:T(8,128)(2,1)S(1)} %get-tuple-element.88), channel_id=1, source_target_pairs={{3,4},{4,3},{7,8},{8,7},{11,12},{12,11},{19,20},{20,19},{23,24},{2... | collective-permute-start | bytes 1572872 | tf_op jit(solution)/shard_map/ppermute | solution.py:476
  29.5 18.2 %collective-permute-start.8 = (bf16[2,512,256]{2,1,0:T(8,128)(2,1)S(1)}, bf16[2,512,256]{2,1,0:T(8,128)(2,1)S(1)}, u32[]{:S(2)}, u32[]{:S(2)}) collective-permute-start(bf16[2,512,256]{2,1,0:T(8,128)(2,1)S(1)} %get-tuple-element.88), channel_id=1, source_target_pairs={{1,2},{2,1},{5,6},{6,5},{9,10},{10,9},{13,14},{14,13},{17,18},{18,... | collective-permute-start | bytes 1572872 | tf_op jit(solution)/shard_map/ppermute | solution.py:476
  30.2 11.2 %collective-permute-start.7 = (bf16[192,256]{1,0:T(8,128)(2,1)S(1)}, bf16[192,256]{1,0:T(8,128)(2,1)S(1)}, u32[]{:S(2)}, u32[]{:S(2)}) collective-permute-start(bf16[192,256]{1,0:T(8,128)(2,1)S(1)} %add.4.refs_0_), channel_id=1, source_target_pairs={{0,10},{1,11},{2,8},{3,9},{4,14},{5,15},{6,12},{7,13},{8,2},{9,3},... | collective-permute-start | bytes 294920 | tf_op jit(solution)/shard_map/ppermute | solution.py:283
  35.0 9.3 %collective-permute-start.6 = (bf16[192,256]{1,0:T(8,128)(2,1)S(1)}, bf16[192,256]{1,0:T(8,128)(2,1)S(1)}, u32[]{:S(2)}, u32[]{:S(2)}) collective-permute-start(bf16[192,256]{1,0:T(8,128)(2,1)S(1)} %add.4.refs_0_), channel_id=1, source_target_pairs={{0,2},{1,3},{2,0},{3,1},{4,6},{5,7},{6,4},{7,5},{8,10},{9,11},{10,... | collective-permute-start | bytes 294920 | tf_op jit(solution)/shard_map/ppermute | solution.py:283
  35.0 11.2 %collective-permute-start.5 = (bf16[192,256]{1,0:T(8,128)(2,1)S(1)}, bf16[192,256]{1,0:T(8,128)(2,1)S(1)}, u32[]{:S(2)}, u32[]{:S(2)}) collective-permute-start(bf16[192,256]{1,0:T(8,128)(2,1)S(1)} %add.4.refs_0_), channel_id=1, source_target_pairs={{0,8},{1,9},{2,10},{3,11},{4,12},{5,13},{6,14},{7,15},{8,0},{9,1},... | collective-permute-start | bytes 294920 | tf_op jit(solution)/shard_map/ppermute | solution.py:283
  46.3 5.1 %collective-permute-start.10 = (bf16[192,256]{1,0:T(8,128)(2,1)S(1)}, bf16[192,256]{1,0:T(8,128)(2,1)S(1)}, u32[]{:S(2)}, u32[]{:S(2)}) collective-permute-start(bf16[192,256]{1,0:T(8,128)(2,1)S(1)} %add.5.mine), channel_id=1, source_target_pairs={{0,4},{1,5},{2,6},{3,7},{4,0},{5,1},{6,2},{7,3},{8,12},{9,13},{10,... | collective-permute-start | bytes 294920 | tf_op jit(solution)/shard_map/ppermute | solution.py:283
  51.4 1.5 %collective-permute-start.11 = (bf16[384,256]{1,0:T(8,128)(2,1)S(1)}, bf16[384,256]{1,0:T(8,128)(2,1)S(1)}, u32[]{:S(2)}, u32[]{:S(2)}) collective-permute-start(bf16[384,256]{1,0:T(8,128)(2,1)S(1)} %join.1.mine), channel_id=1, source_target_pairs={{0,1},{1,0},{2,3},{3,2},{4,5},{5,4},{6,7},{7,6},{8,9},{9,8},{10,11... | collective-permute-start | bytes 589832 | tf_op jit(solution)/shard_map/ppermute | solution.py:283
